TPU v7x, 256 devices: a whole 4x4x8 slice. The times are simulated.
256 devices in a mesh: grp: 8 (over y_lo, x), dev: 32 (over y_hi, z, core).
Axes of the slice: x: 4, y: 4 (y_hi: 2, y_lo: 2; y = y_hi * 2 + y_lo), z: 8, core: 2. Of those that a mesh axis runs over, the one named last changes fastest.
Arguments:
- noise_draws: bfloat16 [16384, 1024], P('dev', 'grp'), may hold values from -12 to 12
- latents: bfloat16 [16384, 1024], P(('grp', 'dev')), may hold values from -6 to 6
Outputs:
- targets: float32 [16384, 1024], P('dev', 'grp')
All inputs are finite; a program needn't handle non-finite values.
Results may differ from a plain program's by a relative error of at most 0.0027.
Values may be sent and summed in bfloat16 or wider, within the bound.
No kernel may reach another device: no remote copies, remote signals or barrier semaphores. Data moves between devices by JAX's collectives and lax.ppermute only.
A program may use at most 64 MiB of HBM per device.

v0:
```python
import functools
import math

import jax
import jax.numpy as jnp
from jax import lax
from jax.experimental import pallas as pl
from jax.experimental.pallas import tpu as pltpu
from jax.sharding import Mesh
from jax.sharding import PartitionSpec as P


ITERS = 4
AXES = ("y_lo", "x", "y_hi", "z", "core")
SIZES = (2, 4, 2, 8, 2)
ROW = ("y_lo", "x", "core")
COL = ("y_hi", "z")
OWNERS = ("x", "y_lo")
BLOCKS = (0, 4, 1, 5, 2, 6, 3, 7)
FEATURES = 1024
ROWS = 1024
COLS = 1024
SAMPLES = 16384
STEP = 128
TINY = 2.0**-90
LARGE = 2.0**100
SHIFT = math.log2(SAMPLES)
SCALE = math.sqrt(FEATURES) * math.log2(math.e)
VMEM = pl.BlockSpec(memory_space=pltpu.VMEM)
SMEM = pl.BlockSpec(memory_space=pltpu.SMEM)
F32 = jnp.float32
BF16 = jnp.bfloat16


def call(kernel, out, scratch=(), flops=0, scalars=0, arrays=0, limit=8, aliases=None, kept=()):
    return pl.pallas_call(
        kernel,
        out_shape=out,
        in_specs=[
            pl.BlockSpec(memory_space=pl.ANY) if k in kept else SMEM if k < scalars else VMEM
            for k in range(scalars + arrays)
        ],
        out_specs=jax.tree.map(lambda _: VMEM, out),
        scratch_shapes=list(scratch),
        input_output_aliases=aliases or {},
        compiler_params=pltpu.CompilerParams(vmem_limit_bytes=limit << 20),
        cost_estimate=pl.CostEstimate(flops=flops, bytes_accessed=4 << 20, transcendentals=1 << 20),
    )


def diagonal():
    return lax.broadcasted_iota(jnp.int32, (128, 128), 0) == lax.broadcasted_iota(
        jnp.int32, (128, 128), 1
    )


def to_lanes(column, eye):
    parts = []
    for k in range(column.shape[0] // 128):
        spread = jnp.broadcast_to(column[k * 128 : (k + 1) * 128], (128, 128))
        parts.append(jnp.sum(jnp.where(eye, spread, 0.0), axis=0, keepdims=True))
    return jnp.concatenate(parts, axis=0)


def to_sublanes(line):
    return jnp.broadcast_to(line, (128, 128)).T


def joined_lse(parts):
    top = jnp.max(parts, axis=0)
    return top + jnp.log2(jnp.sum(jnp.exp2(parts - top[None]), axis=0))


def row_part(tile_ref, dual, out_ref, lse_ref):
    lines = [jnp.broadcast_to(dual[k : k + 1], (8, 128)) for k in range(8)]
    step = 64

    @pl.loop(0, ROWS // step)
    def _(at):
        rows = pl.ds(pl.multiple_of(at * step, step), step)
        logits = [
            tile_ref[rows, k * 128 : (k + 1) * 128] + jnp.tile(lines[k], (step // 8, 1))
            for k in range(8)
        ]
        top = logits[0]
        for part in logits[1:]:
            top = jnp.maximum(top, part)
        top = jnp.max(top, axis=1, keepdims=True)
        mass = jnp.exp2(logits[0] - top)
        for part in logits[1:]:
            mass = mass + jnp.exp2(part - top)
        mass = jnp.sum(mass, axis=1, keepdims=True)
        lse_ref[rows, :] = jnp.broadcast_to(top + jnp.log2(mass), (step, 128))

    out_ref[...] = jnp.broadcast_to(to_lanes(lse_ref[...], diagonal())[None], out_ref.shape)


def column_part(tile_ref, dual, out_ref, dual_ref):
    for k in range(8):
        dual_ref[k * 128 : (k + 1) * 128, :] = to_sublanes(dual[k : k + 1])
    step = 32

    def shifted(at, k):
        rows = pl.ds(pl.multiple_of(at * step, step), step)
        return tile_ref[rows, k * 128 : (k + 1) * 128] + dual_ref[rows, :]

    def peak(at, tops):
        return tuple(
            jnp.maximum(top, jnp.max(shifted(at, k).reshape(step // 8, 8, 128), axis=0))
            for k, top in enumerate(tops)
        )

    low = jnp.full((8, 128), -jnp.inf, F32)
    tops = lax.fori_loop(0, ROWS // step, peak, (low,) * 8)
    tops = [jnp.max(top, axis=0, keepdims=True) for top in tops]
    wide = [jnp.broadcast_to(top, (step, 128)) for top in tops]

    def add(at, sums):
        return tuple(
            total + jnp.sum(jnp.exp2(shifted(at, k) - wide[k]).reshape(step // 8, 8, 128), axis=0)
            for k, total in enumerate(sums)
        )

    sums = lax.fori_loop(0, ROWS // step, add, (jnp.zeros((8, 128), F32),) * 8)
    lse = jnp.concatenate(
        [
            top + jnp.log2(jnp.sum(total, axis=0, keepdims=True))
            for top, total in zip(tops, sums)
        ],
        axis=0,
    )
    out_ref[...] = jnp.broadcast_to(lse[None], out_ref.shape)


def lane_sums(wide):
    ones = jnp.ones((8, 128), BF16)
    rest, total = wide, 0.0
    for _ in range(3):
        piece = rest.astype(BF16)
        rest = rest - piece.astype(F32)
        total = total + lax.dot_general(
            ones, piece, (((1,), (1,)), ((), ())), preferred_element_type=F32
        )
    return jnp.concatenate(
        [total[0:1, k * 128 : (k + 1) * 128] for k in range(wide.shape[0] // 128)], axis=0
    )


def row_kernel(terms_ref, tile_ref, parts_ref, base_ref, out_ref, sums_ref):
    dual = -SHIFT - joined_lse(parts_ref[...])
    top = jnp.max(dual)
    factor = jnp.exp2(dual - top)
    lines = [jnp.broadcast_to(factor[k : k + 1], (8, 128)) for k in range(8)]

    @pl.loop(0, ROWS // STEP)
    def _(at):
        for q in range(STEP // 8):
            rows = pl.ds(pl.multiple_of(at * STEP + q * 8, 8), 8)
            mass = None
            for k in range(8):
                term = terms_ref[rows, k * 128 : (k + 1) * 128] * lines[k]
                mass = term if mass is None else mass + term
            sums_ref[rows, :] = mass

    total = lane_sums(sums_ref[...])
    lse = (top - SHIFT) - base_ref[...] + jnp.log2(total)
    out_ref[...] = jnp.broadcast_to(lse[None], out_ref.shape)

    @pl.when(jnp.min(total) < TINY)
    def _():
        row_part(tile_ref, dual, out_ref, sums_ref)


def column_total(sums):
    return jnp.concatenate([jnp.sum(part, axis=0, keepdims=True) for part in sums], axis=0)


def column_kernel(terms_ref, tile_ref, parts_ref, base_ref, out_ref, wide_ref):
    dual = -SHIFT - joined_lse(parts_ref[...])
    change = dual - base_ref[...]
    top = jnp.max(change)
    factor = jnp.exp2(change - top)
    for k in range(8):
        wide_ref[k * 128 : (k + 1) * 128, :] = to_sublanes(factor[k : k + 1])

    def add(at, sums):
        sums = list(sums)
        for q in range(STEP // 8):
            rows = pl.ds(pl.multiple_of(at * STEP + q * 8, 8), 8)
            share = wide_ref[rows, :]
            for k in range(8):
                sums[k] = sums[k] + terms_ref[rows, k * 128 : (k + 1) * 128] * share
        return tuple(sums)

    sums = lax.fori_loop(0, ROWS // STEP, add, (jnp.zeros((8, 128), F32),) * 8)
    total = column_total(sums)
    out_ref[...] = jnp.broadcast_to(((top - SHIFT) + jnp.log2(total))[None], out_ref.shape)

    @pl.when(jnp.min(total) < TINY)
    def _():
        column_part(tile_ref, dual, out_ref, wide_ref)


def first_column_kernel(tile_ref, parts_ref, out_ref, dual_ref, terms_ref, wide_ref):
    dual = -SHIFT - joined_lse(parts_ref[...])
    dual_ref[...] = dual
    for k in range(8):
        wide_ref[k * 128 : (k + 1) * 128, :] = to_sublanes(dual[k : k + 1] + SHIFT)

    def add(at, sums):
        sums = list(sums)
        for q in range(STEP // 8):
            rows = pl.ds(pl.multiple_of(at * STEP + q * 8, 8), 8)
            shift = wide_ref[rows, :]
            for k in range(8):
                here = slice(k * 128, (k + 1) * 128)
                term = jnp.exp2(tile_ref[rows, here] + shift)
                terms_ref[rows, here] = term
                sums[k] = sums[k] + term
        return tuple(sums)

    sums = lax.fori_loop(0, ROWS // STEP, add, (jnp.zeros((8, 128), F32),) * 8)
    total = column_total(sums)
    out_ref[...] = jnp.broadcast_to((jnp.log2(total) - SHIFT)[None], out_ref.shape)

    @pl.when(jnp.min(total) < TINY)
    def _():
        column_part(tile_ref, dual, out_ref, wide_ref)


def noise_kernel(place_ref, parts_ref, rows_ref):
    for k in range(4):
        for other in range(2):
            at = jnp.bitwise_xor(place_ref[0], other) * 4 + k
            rows_ref[:, pl.ds(pl.multiple_of(at * 128, 128), 128)] = parts_ref[k, other]


def spread_kernel(noise_ref, other_ref, out_ref, sems):
    copies = [
        pltpu.make_async_copy(ref, out_ref.at[k, j], sems.at[k, j])
        for j, ref in enumerate((noise_ref, other_ref))
        for k in range(4)
    ]
    for copy in copies:
        copy.start()
    for copy in copies:
        copy.wait()


def pack_kernel(*refs):
    for k, ref in enumerate(refs[:-1]):
        refs[-1][k * 64 : (k + 1) * 64, :] = ref[...]


def squares(ref, rows):
    total = None
    for k in range(8):
        wide = ref[rows, k * 128 : (k + 1) * 128].astype(F32)
        total = wide * wide if total is None else total + wide * wide
    return jnp.sum(total, axis=1, keepdims=True)


def costs(noise, starts, block_ref, tile_ref, squares_ref, base, use):
    eye = diagonal()

    @pl.loop(0, 2)
    def _(at):
        cols = pl.ds(pl.multiple_of(base + at * 256, 256), 256)
        latent_sq = squares(block_ref, cols)
        for start, ref in zip(starts, noise):
            cross = lax.dot_general(
                ref[...], block_ref[cols, :], (((1,), (1,)), ((), ())), preferred_element_type=F32
            )
            rows, pair = pl.ds(start, 512), []
            for k in range(2):
                spread = jnp.broadcast_to(latent_sq[k * 128 : (k + 1) * 128], (128, 128))
                line = jnp.sum(jnp.where(eye, spread, 0.0), axis=0, keepdims=True)
                line = jnp.broadcast_to(line, (512, 128))
                cost = squares_ref[rows, :] + line - 2.0 * cross[:, k * 128 : (k + 1) * 128]
                cost = cost * (-SCALE / FEATURES)
                tile_ref[rows, pl.ds(pl.multiple_of(base + at * 256 + k * 128, 128), 128)] = cost
                pair.append(cost)
            use(at, rows, pair)


def halves(core):
    return [pl.multiple_of(jnp.bitwise_xor(core, half) * 512, 512) for half in range(2)]


def placed(packs, block_ref, group, z, orders):
    for pack, backs in zip(packs, orders):
        for k, back in enumerate(backs):
            at = group * 8 + jnp.bitwise_and(z - back + 8, 7)
            rows = pl.ds(pl.multiple_of(at * 64, 64), 64)
            block_ref[rows, :] = pack[k * 64 : (k + 1) * 64, :]


def first_masses(tile_ref, base, top_ref, sums_ref):
    @pl.loop(0, ROWS // STEP)
    def _(at):
        for q in range(STEP // 8):
            rows = pl.ds(pl.multiple_of(at * STEP + q * 8, 8), 8)
            top = jnp.broadcast_to(jnp.max(top_ref[rows, :], axis=1, keepdims=True), (8, 128))
            top_ref[rows, :] = top
            mass = None
            for k in range(4):
                cols = pl.ds(pl.multiple_of(base + k * 128, 128), 128)
                term = jnp.exp2(tile_ref[rows, cols] - top)
                mass = term if mass is None else mass + term
            sums_ref[rows, :] = mass


def near_kernel(place_ref, *refs):
    noise, own_ref, near = refs[:2], refs[2], refs[3:7]
    block_ref, tile_ref, squares_ref, top_ref, sums_ref, line_ref, sem = refs[7:]
    y_hi, z, core = (place_ref[k] for k in range(2, 5))
    at = pl.multiple_of((y_hi * 8 + z) * 64, 64)
    fetch = pltpu.make_async_copy(own_ref, block_ref.at[pl.ds(at, 64), :], sem)
    fetch.start()
    placed(near, block_ref, y_hi, z, PACKS[1:])
    starts = halves(core)
    for start, ref in zip(starts, noise):
        for k in range(4):
            squares_ref[pl.ds(start + k * 128, 128), :] = jnp.broadcast_to(
                squares(ref, slice(k * 128, (k + 1) * 128)), (128, 128)
            )
    fetch.wait()
    base = pl.multiple_of(y_hi * 512, 512)

    def use(at, rows, pair):
        top = jnp.maximum(*pair)
        top_ref[rows, :] = jnp.maximum(jnp.where(at == 0, top, top_ref[rows, :]), top)

    costs(noise, starts, block_ref, tile_ref, squares_ref, base, use)
    first_masses(tile_ref, base, top_ref, sums_ref)
    line_ref[...] = to_lanes(top_ref[...], diagonal())


def far_kernel(place_ref, *refs):
    noise, far = refs[:2], refs[2:7]
    squares_ref, top_ref, near_sums_ref, line_ref, _, _ = refs[7:13]
    block_ref, tile_ref, out_ref, sums_ref = refs[13:]
    y_hi, z, core = (place_ref[k] for k in range(2, 5))
    placed(far, block_ref, 1 - y_hi, z, PACKS)
    base = pl.multiple_of((1 - y_hi) * 512, 512)
    sums_ref[...] = near_sums_ref[...]

    def use(at, rows, pair):
        top = top_ref[rows, :]
        sums_ref[rows, :] = sums_ref[rows, :] + (jnp.exp2(pair[0] - top) + jnp.exp2(pair[1] - top))

    costs(noise, halves(core), block_ref, tile_ref, squares_ref, base, use)
    largest = jnp.max(sums_ref[...])
    lse = line_ref[...] + jnp.log2(lane_sums(sums_ref[...]))
    out_ref[...] = jnp.broadcast_to(lse[None], out_ref.shape)

    @pl.when(jnp.logical_not(largest < LARGE))
    def _():
        row_part(tile_ref, jnp.zeros((8, 128), F32), out_ref, sums_ref)


def last_kernel(
    mine, skip, core_ref, terms_ref, tile_ref, parts_ref, base_ref, block_ref,
    out_ref, limit_ref, mass_ref, wide_ref, sums_ref, weights_ref,
):
    count = out_ref.shape[0]
    half = core_ref[0] if mine else 1 - core_ref[0]
    first = pl.multiple_of(half * 512 + skip, 128)
    dual = -SHIFT - joined_lse(parts_ref[...])
    top = jnp.max(dual)
    factor = jnp.exp2(dual - top)
    lines = slice(skip // 128, (skip + count) // 128)
    base = jnp.where(half == 0, base_ref[0:4], base_ref[4:8])[lines]

    def keep(start, values):
        mass = None
        for k, term in enumerate(values):
            mass = term if mass is None else mass + term
            weights_ref[pl.ds(start, 16), k * 128 : (k + 1) * 128] = term.astype(BF16)
        sums_ref[pl.ds(start, 16), :] = mass

    shares = [jnp.broadcast_to(factor[k : k + 1], (16, 128)) for k in range(8)]

    @pl.loop(0, count // 128)
    def _(at):
        for q in range(8):
            start = pl.multiple_of(at * 128 + q * 16, 16)
            rows = pl.ds(pl.multiple_of(first + start, 16), 16)
            keep(start, [terms_ref[rows, k * 128 : (k + 1) * 128] * shares[k] for k in range(8)])

    limit_ref[...] = (top - SHIFT) - base
    mass_ref[...] = lane_sums(sums_ref[...])

    @pl.when(jnp.min(mass_ref[...]) < TINY)
    def _():
        duals = [jnp.broadcast_to(dual[k : k + 1], (16, 128)) for k in range(8)]

        @pl.loop(0, count // 16)
        def _(at):
            start = pl.multiple_of(at * 16, 16)
            rows = pl.ds(pl.multiple_of(first + start, 16), 16)
            logits = [tile_ref[rows, k * 128 : (k + 1) * 128] + duals[k] for k in range(8)]
            peak = logits[0]
            for part in logits[1:]:
                peak = jnp.maximum(peak, part)
            peak = jnp.broadcast_to(jnp.max(peak, axis=1, keepdims=True), (16, 128))
            wide_ref[pl.ds(start, 16), :] = peak
            keep(start, [jnp.exp2(part - peak) for part in logits])

        limit_ref[...] = to_lanes(wide_ref[...], diagonal())
        mass_ref[...] = lane_sums(sums_ref[...])

    @pl.loop(0, 4)
    def _(at):
        here = pl.ds(pl.multiple_of(at * 256, 256), 256)
        out_ref[:, here] = jnp.dot(
            weights_ref[...], block_ref[:, here], preferred_element_type=F32
        ).astype(out_ref.dtype)


def pieces_of(value):
    pieces = []
    for _ in range(3):
        pieces.append(value.astype(BF16))
        value = value - pieces[-1].astype(F32)
    return pieces


def cores_kernel(
    skip, mine_ref, limit_ref, mass_ref, other_ref, other_limit_ref, other_mass_ref, out_ref
):
    count = mine_ref.shape[0]
    lines = slice(skip // 128, (skip + count) // 128)
    other_limit, other_mass = other_limit_ref[...][lines], other_mass_ref[...][lines]
    limit = jnp.maximum(limit_ref[...], other_limit)
    a, b = jnp.exp2(limit_ref[...] - limit), jnp.exp2(other_limit - limit)
    mass = a * mass_ref[...] + b * other_mass
    for k in range(count // 128):
        wide_a, wide_b = to_sublanes(a[k : k + 1]), to_sublanes(b[k : k + 1])
        rows = slice(k * 128, (k + 1) * 128)
        other_rows = slice(skip + k * 128, skip + (k + 1) * 128)
        for g, block in enumerate(BLOCKS):
            here = slice(block * 128, (block + 1) * 128)
            out_ref[g, rows, :] = (
                wide_a * mine_ref[rows, here] + wide_b * other_ref[other_rows, here].astype(F32)
            ).astype(BF16)
    pieces = pieces_of(limit) + pieces_of(mass)
    pieces = jnp.concatenate(pieces + [jnp.zeros_like(pieces[0])] * 2, axis=0)
    for g in range(8):
        out_ref[g, count:, :] = pieces


def groups_kernel(*refs):
    out_ref, start = refs[-1], 0
    for parts_ref in refs[:-1]:
        count = parts_ref.shape[1] // 136 * 128
        n = count // 128
        pieces = parts_ref[:, count:, :].astype(F32)
        limit = pieces[:, 0:n] + pieces[:, n : 2 * n] + pieces[:, 2 * n : 3 * n]
        mass = pieces[:, 3 * n : 4 * n] + pieces[:, 4 * n : 5 * n] + pieces[:, 5 * n : 6 * n]
        share = jnp.exp2(limit - jnp.max(limit, axis=0)[None])
        share = share / jnp.sum(share * mass, axis=0)[None]
        for k in range(n):
            total = jnp.zeros((128, 128), F32)
            for g in range(8):
                total = total + to_sublanes(share[g, k : k + 1]) * parts_ref[
                    g, k * 128 : (k + 1) * 128, :
                ].astype(F32)
            out_ref[start + k * 128 : start + (k + 1) * 128, :] = total
        start += count


def moved(array, axis, step):
    size = lax.axis_size(axis)
    return lax.ppermute(array, axis, [(k, (k + step) % size) for k in range(size)])


def exchanged(parts, axes):
    return lax.all_to_all(parts, axes, 0, 0, tiled=True)


def local(noise_draws, latents):
    place = jnp.stack([lax.axis_index(axis) for axis in AXES]).astype(jnp.int32)
    part = jax.ShapeDtypeStruct((16, 8, 128), F32)
    line = jax.ShapeDtypeStruct((8, 128), F32)
    wide = pltpu.VMEM((ROWS, 128), F32)

    block_out = jax.ShapeDtypeStruct((COLS, FEATURES), BF16)
    tile_out = jax.ShapeDtypeStruct((ROWS, COLS), F32)
    wide_out = jax.ShapeDtypeStruct((ROWS, 128), F32)

    near, far = [latents] + [None] * 7, []
    near[1] = moved(latents, "z", 1)
    near[7] = moved(latents, "z", -1)
    near[2] = moved(near[1], "z", 1)
    near[6] = moved(near[7], "z", -1)
    near[3] = moved(near[2], "z", 1)
    near[5] = moved(near[6], "z", -1)
    near[4] = moved(near[2], "z", 2)
    packs = []
    for backs in PACKS:
        if len(backs) == 1:
            packs.append(near[backs[0]])
            continue
        packs.append(
            call(
                pack_kernel,
                jax.ShapeDtypeStruct((64 * len(backs), FEATURES), BF16),
                arrays=len(backs),
                limit=2,
            )(*(near[back] for back in backs))
        )
    far = [moved(pack, "y_hi", 1) for pack in packs]
    noise_pair = moved(noise_draws, "y_lo", 1)
    spread = pl.pallas_call(
        spread_kernel,
        out_shape=jax.ShapeDtypeStruct((4, 2, *noise_draws.shape), BF16),
        in_specs=[VMEM, VMEM],
        out_specs=pl.BlockSpec(memory_space=pl.ANY),
        scratch_shapes=[pltpu.SemaphoreType.DMA((4, 2))],
        name="spread",
        compiler_params=pltpu.CompilerParams(vmem_limit_bytes=2 << 20),
    )(noise_draws, noise_pair)
    features = exchanged(spread, "x")
    rows = call(
        noise_kernel, jax.ShapeDtypeStruct((512, FEATURES), BF16), scalars=1, arrays=1, limit=4
    )(place, features)
    other_rows = moved(rows, "core", 1)
    block, tile, squared, top, masses, peaks = call(
        near_kernel,
        (block_out, tile_out, wide_out, wide_out, wide_out, line),
        [pltpu.SemaphoreType.DMA],
        flops=1 << 30,
        scalars=1,
        arrays=7,
        kept=(3,),
    )(place, rows, other_rows, *packs)
    block, tile, parts = call(
        far_kernel, (block_out, tile_out, part), [wide], 1 << 30, 1, 13, aliases={12: 0, 13: 1}
    )(place, rows, other_rows, *far, squared, top, masses, peaks, block, tile)
    for sweep in range(ITERS):
        if sweep:
            parts = call(row_kernel, part, [wide], arrays=4)(terms, tile, parts, base)
        parts = exchanged(parts, ROW)
        if sweep:
            parts = call(column_kernel, part, [wide], arrays=4)(terms, tile, parts, base)
        else:
            parts, base, terms = call(
                first_column_kernel, (part, line, tile_out), [wide], arrays=2
            )(tile, parts)
        parts = exchanged(parts, COL)
    core = place[4:5]

    def last(mine, skip, count, dtype):
        lines = jax.ShapeDtypeStruct((count // 128, 128), F32)
        spare = pltpu.VMEM((count, 128), F32)
        return call(
            functools.partial(last_kernel, mine, skip),
            (jax.ShapeDtypeStruct((count, FEATURES), dtype), lines, lines),
            [spare, spare, pltpu.VMEM((count, COLS), BF16)],
            count << 21,
            1,
            5,
        )(core, terms, tile, parts, base, block)

    away = last(False, 0, 512, BF16)
    other = [moved(value, "core", 1) for value in away]
    messages, skip = [], 0
    for count in OWN:
        own = last(True, skip, count, F32)
        message = call(
            functools.partial(cores_kernel, skip),
            jax.ShapeDtypeStruct((8, count // 128 * 136, 128), BF16),
            arrays=6,
        )(*own, *other)
        messages.append(exchanged(message, OWNERS))
        skip += count
    return call(
        groups_kernel, jax.ShapeDtypeStruct((512, 128), F32), arrays=len(messages)
    )(*messages)


OWN = (512,)
PACKS = ((0,), (1, 7), (2, 6), (3, 5), (4,))


def solution(mesh):
    torus = Mesh(mesh.devices.reshape(SIZES), AXES)
    rows = P(("y_hi", "z", "core"), ("y_lo", "x"))
    return jax.shard_map(
        local, mesh=torus, in_specs=(rows, P(AXES, None)), out_specs=rows, check_vma=False
    )
```

profile of v0, /device:TPU:2, one launch (start us, length us, event | category | flops | bytes accessed | tf_op | source)
XLA Modules:
  0.0 222.8 jit_solution(12781318344314248279)
XLA Ops:
  1.6 3.9 %collective-permute-done.other_ref = bf16[512,128]{1,0:T(8,128)(2,1)S(1)} collective-permute-done((bf16[512,128]{1,0:T(8,128)(2,1)}, bf16[512,128]{1,0:T(8,128)(2,1)S(1)}, u32[]{:S(2)}, u32[]{:S(2)}) %collective-permute-start) | collective-permute-done | bytes 131104 | tf_op jit(solution)/shard_map/ppermute | solution.py:475
  7.4 5.6 %all-to-all-start = ((bf16[4,2,512,128]{3,2,1,0:T(8,128)(2,1)}), bf16[4,2,512,128]{3,2,1,0:T(8,128)(2,1)S(1)}, u32[]{:S(2)}, u32[]{:S(2)}) async-start(bf16[4,2,512,128]{3,2,1,0:T(8,128)(2,1)} %spread.1), calls=%async_computation | async-start | bytes 2097152 | tf_op jit(solution)/shard_map/all_to_all | solution.py:479
  13.1 12.1 %all-to-all-done.parts_ref = bf16[4,2,512,128]{3,2,1,0:T(8,128)(2,1)S(1)} async-done(((bf16[4,2,512,128]{3,2,1,0:T(8,128)(2,1)}), bf16[4,2,512,128]{3,2,1,0:T(8,128)(2,1)S(1)}, u32[]{:S(2)}, u32[]{:S(2)}) %all-to-all-start) | async-done | bytes 1048608 | tf_op jit(solution)/shard_map/all_to_all | solution.py:479
  28.1 4.0 %collective-permute-start.4 = (bf16[64,1024]{1,0:T(8,128)(2,1)S(1)}, bf16[64,1024]{1,0:T(8,128)(2,1)S(1)}, u32[]{:S(2)}, u32[]{:S(2)}) collective-permute-start(bf16[64,1024]{1,0:T(8,128)(2,1)S(1)} %copy-done.1), channel_id=1, source_target_pairs={{0,14},{2,0},{4,2},{6,4},{8,6},{10,8},{12,10},{14,12},{1,15},{3,1}... | collective-permute-start | bytes 393224 | tf_op jit(solution)/shard_map/ppermute | solution.py:475
  32.2 4.0 %collective-permute-done.3.refs_0_ = bf16[64,1024]{1,0:T(8,128)(2,1)S(1)} collective-permute-done((bf16[64,1024]{1,0:T(8,128)(2,1)S(1)}, bf16[64,1024]{1,0:T(8,128)(2,1)S(1)}, u32[]{:S(2)}, u32[]{:S(2)}) %collective-permute-start.3) | collective-permute-done | bytes 131104 | tf_op jit(solution)/shard_map/ppermute | solution.py:475
  36.2 3.2 %collective-permute-start.7 = (bf16[64,1024]{1,0:T(8,128)(2,1)S(1)}, bf16[64,1024]{1,0:T(8,128)(2,1)S(1)}, u32[]{:S(2)}, u32[]{:S(2)}) collective-permute-start(bf16[64,1024]{1,0:T(8,128)(2,1)S(1)} %collective-permute-done.4.refs_1_), channel_id=1, source_target_pairs={{0,14},{2,0},{4,2},{6,4},{8,6},{10,8},{12,10},{14,12},{1,15},{3,1}... | collective-permute-start | bytes 393224 | tf_op jit(solution)/shard_map/ppermute | solution.py:475
  39.4 3.2 %collective-permute-done.6.refs_0_ = bf16[64,1024]{1,0:T(8,128)(2,1)S(1)} collective-permute-done((bf16[64,1024]{1,0:T(8,128)(2,1)S(1)}, bf16[64,1024]{1,0:T(8,128)(2,1)S(1)}, u32[]{:S(2)}, u32[]{:S(2)}) %collective-permute-start.6) | collective-permute-done | bytes 131104 | tf_op jit(solution)/shard_map/ppermute | solution.py:475
  42.6 3.2 %collective-permute-start.10 = (bf16[64,1024]{1,0:T(8,128)(2,1)S(1)}, bf16[64,1024]{1,0:T(8,128)(2,1)S(1)}, u32[]{:S(2)}, u32[]{:S(2)}) collective-permute-start(bf16[64,1024]{1,0:T(8,128)(2,1)S(1)} %collective-permute-done.7.refs_1_), channel_id=1, source_target_pairs={{0,14},{2,0},{4,2},{6,4},{8,6},{10,8},{12,10},{14,12},{1,15},{3,1}... | collective-permute-start | bytes 393224 | tf_op jit(solution)/shard_map/ppermute | solution.py:475
  45.9 3.3 %collective-permute-start.5 = (bf16[128,1024]{1,0:T(8,128)(2,1)S(1)}, bf16[128,1024]{1,0:T(8,128)(2,1)S(1)}, u32[]{:S(2)}, u32[]{:S(2)}) collective-permute-start(bf16[128,1024]{1,0:T(8,128)(2,1)S(1)} %shard_map.29.refs_3_), channel_id=1, source_target_pairs={{0,16},{16,0},{1,17},{17,1},{2,18},{18,2},{3,19},{19,3},{4,20},{20... | collective-permute-start | bytes 786440 | tf_op jit(solution)/shard_map/ppermute | solution.py:475
  49.2 4.6 %collective-permute-start.8 = (bf16[128,1024]{1,0:T(8,128)(2,1)S(1)}, bf16[128,1024]{1,0:T(8,128)(2,1)S(1)}, u32[]{:S(2)}, u32[]{:S(2)}) collective-permute-start(bf16[128,1024]{1,0:T(8,128)(2,1)S(1)} %shard_map.30.refs_4_), channel_id=1, source_target_pairs={{0,16},{16,0},{1,17},{17,1},{2,18},{18,2},{3,19},{19,3},{4,20},{20... | collective-permute-start | bytes 786440 | tf_op jit(solution)/shard_map/ppermute | solution.py:475
  53.9 2.5 %collective-permute-done.12.refs_6_ = bf16[64,1024]{1,0:T(8,128)(2,1)S(1)} collective-permute-done((bf16[64,1024]{1,0:T(8,128)(2,1)S(1)}, bf16[64,1024]{1,0:T(8,128)(2,1)S(1)}, u32[]{:S(2)}, u32[]{:S(2)}) %collective-permute-start.12) | collective-permute-done | bytes 131104 | tf_op jit(solution)/shard_map/ppermute | solution.py:475
  57.4 2.5 %collective-permute-start.13 = (bf16[64,1024]{1,0:T(8,128)(2,1)S(1)}, bf16[64,1024]{1,0:T(8,128)(2,1)S(1)}, u32[]{:S(2)}, u32[]{:S(2)}) collective-permute-start(bf16[64,1024]{1,0:T(8,128)(2,1)S(1)} %collective-permute-done.12.refs_6_), channel_id=1, source_target_pairs={{0,16},{16,0},{1,17},{17,1},{2,18},{18,2},{3,19},{19,3},{4,20},{20... | collective-permute-start | bytes 393224 | tf_op jit(solution)/shard_map/ppermute | solution.py:475
  60.0 4.1 %shard_map.32 = (bf16[1024,1024]{1,0:T(8,128)(2,1)S(1)}, f32[1024,1024]{1,0:T(8,128)S(1)}, f32[1024,128]{1,0:T(8,128)S(1)}, f32[1024,128]{1,0:T(8,128)S(1)}, f32...) custom-call(s32[5]{0:T(128)S(1)} %stack.23.place_ref, bf16[512,1024]{1,0:T(8,128)(2,1)S(1)} %shard_map.28.refs_0_, ...), custom_call_target="tpu_custom_call" | custom-call | flops 1073741824 | bytes 4194304 | tf_op jit(solution)/shard_map/pallas_call | solution.py:529
  64.0 5.5 %collective-permute-done.2.refs_2_ = bf16[64,1024]{1,0:T(8,128)(2,1)S(1)} collective-permute-done((bf16[64,1024]{1,0:T(8,128)(2,1)S(1)}, bf16[64,1024]{1,0:T(8,128)(2,1)S(1)}, u32[]{:S(2)}, u32[]{:S(2)}) %collective-permute-start.2) | collective-permute-done | bytes 131104 | tf_op jit(solution)/shard_map/ppermute | solution.py:475
  70.9 3.0 %shard_map.33 = (bf16[1024,1024]{1,0:T(8,128)(2,1)S(1)}, f32[1024,1024]{1,0:T(8,128)S(1)}, f32[16,8,128]{2,1,0:T(8,128)S(1)}) custom-call(s32[5]{0:T(128)S(1)} %stack.23.place_ref, bf16[512,1024]{1,0:T(8,128)(2,1)S(1)} %shard_map.28.refs_0_, bf16[512,1024]{1,0:T(8,128)(2,1)S(1)} %collective-permute-done.1.refs_1_, ...), custom_call_target="tpu_custom_call", output_to_operand_aliasing={{0}: (12, {}), {1}: (13, {})} | custom-call | flops 1073741824 | bytes 4194304 | tf_op jit(solution)/shard_map/pallas_call | solution.py:538
  74.0 9.5 %all_to_all.50.parts_ref = f32[16,8,128]{2,1,0:T(8,128)S(1)} all-to-all(f32[16,8,128]{2,1,0:T(8,128)S(1)} %get-tuple-element.30), channel_id=1, replica_groups=mesh['y_lo'=2,'x'=4,'y_hi'=2,'z'=8,'core'=2] {'y_lo','x','core'}, dimensions={0} | all-to-all | bytes 131072 | tf_op jit(solution)/shard_map/all_to_all | solution.py:479
  83.4 2.9 %shard_map.34 = (f32[16,8,128]{2,1,0:T(8,128)S(1)}, f32[8,128]{1,0:T(8,128)S(1)}, f32[1024,1024]{1,0:T(8,128)S(1)}) custom-call(f32[1024,1024]{1,0:T(8,128)S(1)} %get-tuple-element.29.tile_ref, f32[16,8,128]{2,1,0:T(8,128)S(1)} %all_to_all.50.parts_ref), custom_call_target="tpu_custom_call" | custom-call | bytes 4194304 | tf_op jit(solution)/shard_map/pallas_call | solution.py:548
  86.4 17.0 %all_to_all.51.parts_ref = f32[16,8,128]{2,1,0:T(8,128)S(1)} all-to-all(f32[16,8,128]{2,1,0:T(8,128)S(1)} %get-tuple-element.32), channel_id=1, replica_groups=mesh['y_lo'=2,'x'=4,'y_hi'=2,'z'=8,'core'=2] {'y_hi','z'}, dimensions={0} | all-to-all | bytes 131072 | tf_op jit(solution)/shard_map/all_to_all | solution.py:479
  103.4 4.4 %shard_map.35 = f32[16,8,128]{2,1,0:T(8,128)S(1)} custom-call(f32[1024,1024]{1,0:T(8,128)S(1)} %get-tuple-element.31.terms_ref, f32[1024,1024]{1,0:T(8,128)S(1)} %get-tuple-element.29.tile_ref, f32[16,8,128]{2,1,0:T(8,128)S(1)} %all_to_all.51.parts_ref, f32[8,128]{1,0:T(8,128)S(1)} %get-tuple-element.33.base_ref), custom_call_target="tpu_custom_call" | custom-call | bytes 4194304 | tf_op jit(solution)/shard_map/pallas_call | solution.py:543
  107.7 8.7 %all_to_all.52.parts_ref = f32[16,8,128]{2,1,0:T(8,128)S(1)} all-to-all(f32[16,8,128]{2,1,0:T(8,128)S(1)} %shard_map.35), channel_id=1, replica_groups=mesh['y_lo'=2,'x'=4,'y_hi'=2,'z'=8,'core'=2] {'y_lo','x','core'}, dimensions={0} | all-to-all | bytes 131072 | tf_op jit(solution)/shard_map/all_to_all | solution.py:479
  116.4 2.5 %shard_map.36 = f32[16,8,128]{2,1,0:T(8,128)S(1)} custom-call(f32[1024,1024]{1,0:T(8,128)S(1)} %get-tuple-element.31.terms_ref, f32[1024,1024]{1,0:T(8,128)S(1)} %get-tuple-element.29.tile_ref, f32[16,8,128]{2,1,0:T(8,128)S(1)} %all_to_all.52.parts_ref, f32[8,128]{1,0:T(8,128)S(1)} %get-tuple-element.33.base_ref), custom_call_target="tpu_custom_call" | custom-call | bytes 4194304 | tf_op jit(solution)/shard_map/pallas_call | solution.py:546
  118.9 12.6 %all_to_all.53.parts_ref = f32[16,8,128]{2,1,0:T(8,128)S(1)} all-to-all(f32[16,8,128]{2,1,0:T(8,128)S(1)} %shard_map.36), channel_id=1, replica_groups=mesh['y_lo'=2,'x'=4,'y_hi'=2,'z'=8,'core'=2] {'y_hi','z'}, dimensions={0} | all-to-all | bytes 131072 | tf_op jit(solution)/shard_map/all_to_all | solution.py:479
  131.6 4.4 %shard_map.37 = f32[16,8,128]{2,1,0:T(8,128)S(1)} custom-call(f32[1024,1024]{1,0:T(8,128)S(1)} %get-tuple-element.31.terms_ref, f32[1024,1024]{1,0:T(8,128)S(1)} %get-tuple-element.29.tile_ref, f32[16,8,128]{2,1,0:T(8,128)S(1)} %all_to_all.53.parts_ref, f32[8,128]{1,0:T(8,128)S(1)} %get-tuple-element.33.base_ref), custom_call_target="tpu_custom_call" | custom-call | bytes 4194304 | tf_op jit(solution)/shard_map/pallas_call | solution.py:543
  136.0 8.7 %all_to_all.54.parts_ref = f32[16,8,128]{2,1,0:T(8,128)S(1)} all-to-all(f32[16,8,128]{2,1,0:T(8,128)S(1)} %shard_map.37), channel_id=1, replica_groups=mesh['y_lo'=2,'x'=4,'y_hi'=2,'z'=8,'core'=2] {'y_lo','x','core'}, dimensions={0} | all-to-all | bytes 131072 | tf_op jit(solution)/shard_map/all_to_all | solution.py:479
  144.6 2.5 %shard_map.38 = f32[16,8,128]{2,1,0:T(8,128)S(1)} custom-call(f32[1024,1024]{1,0:T(8,128)S(1)} %get-tuple-element.31.terms_ref, f32[1024,1024]{1,0:T(8,128)S(1)} %get-tuple-element.29.tile_ref, f32[16,8,128]{2,1,0:T(8,128)S(1)} %all_to_all.54.parts_ref, f32[8,128]{1,0:T(8,128)S(1)} %get-tuple-element.33.base_ref), custom_call_target="tpu_custom_call" | custom-call | bytes 4194304 | tf_op jit(solution)/shard_map/pallas_call | solution.py:546
  147.1 12.9 %all_to_all.55.parts_ref = f32[16,8,128]{2,1,0:T(8,128)S(1)} all-to-all(f32[16,8,128]{2,1,0:T(8,128)S(1)} %shard_map.38), channel_id=1, replica_groups=mesh['y_lo'=2,'x'=4,'y_hi'=2,'z'=8,'core'=2] {'y_hi','z'}, dimensions={0} | all-to-all | bytes 131072 | tf_op jit(solution)/shard_map/all_to_all | solution.py:479
  160.0 4.4 %shard_map.39 = f32[16,8,128]{2,1,0:T(8,128)S(1)} custom-call(f32[1024,1024]{1,0:T(8,128)S(1)} %get-tuple-element.31.terms_ref, f32[1024,1024]{1,0:T(8,128)S(1)} %get-tuple-element.29.tile_ref, f32[16,8,128]{2,1,0:T(8,128)S(1)} %all_to_all.55.parts_ref, f32[8,128]{1,0:T(8,128)S(1)} %get-tuple-element.33.base_ref), custom_call_target="tpu_custom_call" | custom-call | bytes 4194304 | tf_op jit(solution)/shard_map/pallas_call | solution.py:543
  164.4 8.7 %all_to_all.56.parts_ref = f32[16,8,128]{2,1,0:T(8,128)S(1)} all-to-all(f32[16,8,128]{2,1,0:T(8,128)S(1)} %shard_map.39), channel_id=1, replica_groups=mesh['y_lo'=2,'x'=4,'y_hi'=2,'z'=8,'core'=2] {'y_lo','x','core'}, dimensions={0} | all-to-all | bytes 131072 | tf_op jit(solution)/shard_map/all_to_all | solution.py:479
  175.6 12.6 %all_to_all.57.parts_ref = f32[16,8,128]{2,1,0:T(8,128)S(1)} all-to-all(f32[16,8,128]{2,1,0:T(8,128)S(1)} %shard_map.40), channel_id=1, replica_groups=mesh['y_lo'=2,'x'=4,'y_hi'=2,'z'=8,'core'=2] {'y_hi','z'}, dimensions={0} | all-to-all | bytes 131072 | tf_op jit(solution)/shard_map/all_to_all | solution.py:479
  188.2 6.2 %shard_map.42 = (bf16[512,1024]{1,0:T(8,128)(2,1)S(1)}, f32[4,128]{1,0:T(4,128)S(1)}, f32[4,128]{1,0:T(4,128)S(1)}) custom-call(s32[1]{0:T(128)} %bitcast.core_ref, f32[1024,1024]{1,0:T(8,128)S(1)} %get-tuple-element.31.terms_ref, f32[1024,1024]{1,0:T(8,128)S(1)} %get-tuple-element.29.tile_ref, f32[16,8,128]{2,1,0:T(8,128)S(1)} %all_to_all.57.parts_ref, ...), custom_call_target="tpu_custom_call" | custom-call | flops 1073741824 | bytes 4194304 | tf_op jit(solution)/shard_map/pallas_call | solution.py:557
  195.1 6.2 %shard_map.41 = (f32[512,1024]{1,0:T(8,128)S(1)}, f32[4,128]{1,0:T(4,128)S(1)}, f32[4,128]{1,0:T(4,128)S(1)}) custom-call(s32[1]{0:T(128)} %bitcast.core_ref, f32[1024,1024]{1,0:T(8,128)S(1)} %get-tuple-element.31.terms_ref, f32[1024,1024]{1,0:T(8,128)S(1)} %get-tuple-element.29.tile_ref, f32[16,8,128]{2,1,0:T(8,128)S(1)} %all_to_all.57.parts_ref, ...), custom_call_target="tpu_custom_call" | custom-call | flops 1073741824 | bytes 4194304 | tf_op jit(solution)/shard_map/pallas_call | solution.py:557
  201.7 19.7 %all_to_all.58.refs_0_ = bf16[8,544,128]{2,1,0:T(8,128)(2,1)S(1)} all-to-all(bf16[8,544,128]{2,1,0:T(8,128)(2,1)S(1)} %shard_map.43), channel_id=1, replica_groups=mesh['y_lo'=2,'x'=4,'y_hi'=2,'z'=8,'core'=2] {'x','y_lo'}, dimensions={0} | all-to-all | bytes 2228224 | tf_op jit(solution)/shard_map/all_to_all | solution.py:479
  (36 shorter events, 14.0 us)
Async XLA Ops:
  0.0 5.4 %collective-permute-start = (bf16[512,128]{1,0:T(8,128)(2,1)}, bf16[512,128]{1,0:T(8,128)(2,1)S(1)}, u32[]{:S(2)}, u32[]{:S(2)}) collective-permute-start(bf16[512,128]{1,0:T(8,128)(2,1)} %noise_ref.1), channel_id=1, source_target_pairs={{0,128},{128,0},{1,129},{129,1},{2,130},{130,2},{3,131},{131,3},{4... | collective-permute-start | bytes 393224 | tf_op jit(solution)/shard_map/ppermute | solution.py:475
  5.4 0.9 copy-start
  7.4 18.7 %copy-start.1 = (bf16[64,1024]{1,0:T(8,128)(2,1)S(1)}, bf16[64,1024]{1,0:T(8,128)(2,1)}, u32[]{:S(2)}) copy-start(bf16[64,1024]{1,0:T(8,128)(2,1)} %refs_2_.1) | copy-start | bytes 393220
  7.4 17.8 %all-to-all-start = ((bf16[4,2,512,128]{3,2,1,0:T(8,128)(2,1)}), bf16[4,2,512,128]{3,2,1,0:T(8,128)(2,1)S(1)}, u32[]{:S(2)}, u32[]{:S(2)}) async-start(bf16[4,2,512,128]{3,2,1,0:T(8,128)(2,1)} %spread.1), calls=%async_computation | async-start | bytes 2097152 | tf_op jit(solution)/shard_map/all_to_all | solution.py:479
  26.0 31.4 %collective-permute-start.1 = (bf16[512,1024]{1,0:T(8,128)(2,1)S(1)}, bf16[512,1024]{1,0:T(8,128)(2,1)S(1)}, u32[]{:S(2)}, u32[]{:S(2)}) collective-permute-start(bf16[512,1024]{1,0:T(8,128)(2,1)S(1)} %shard_map.28.refs_0_), channel_id=1, source_target_pairs={{0,1},{1,0},{2,3},{3,2},{4,5},{5,4},{6,7},{7,6},{8,9},{9,8},{10,11... | collective-permute-start | bytes 3145736 | tf_op jit(solution)/shard_map/ppermute | solution.py:475
  26.1 10.0 %collective-permute-start.3 = (bf16[64,1024]{1,0:T(8,128)(2,1)S(1)}, bf16[64,1024]{1,0:T(8,128)(2,1)S(1)}, u32[]{:S(2)}, u32[]{:S(2)}) collective-permute-start(bf16[64,1024]{1,0:T(8,128)(2,1)S(1)} %copy-done.1), channel_id=1, source_target_pairs={{0,2},{2,4},{4,6},{6,8},{8,10},{10,12},{12,14},{14,0},{1,3},{3,5},... | collective-permute-start | bytes 393224 | tf_op jit(solution)/shard_map/ppermute | solution.py:475
  28.1 8.0 %collective-permute-start.4 = (bf16[64,1024]{1,0:T(8,128)(2,1)S(1)}, bf16[64,1024]{1,0:T(8,128)(2,1)S(1)}, u32[]{:S(2)}, u32[]{:S(2)}) collective-permute-start(bf16[64,1024]{1,0:T(8,128)(2,1)S(1)} %copy-done.1), channel_id=1, source_target_pairs={{0,14},{2,0},{4,2},{6,4},{8,6},{10,8},{12,10},{14,12},{1,15},{3,1}... | collective-permute-start | bytes 393224 | tf_op jit(solution)/shard_map/ppermute | solution.py:475
  36.2 6.4 %collective-permute-start.6 = (bf16[64,1024]{1,0:T(8,128)(2,1)S(1)}, bf16[64,1024]{1,0:T(8,128)(2,1)S(1)}, u32[]{:S(2)}, u32[]{:S(2)}) collective-permute-start(bf16[64,1024]{1,0:T(8,128)(2,1)S(1)} %collective-permute-done.3.refs_0_), channel_id=1, source_target_pairs={{0,2},{2,4},{4,6},{6,8},{8,10},{10,12},{12,14},{14,0},{1,3},{3,5},... | collective-permute-start | bytes 393224 | tf_op jit(solution)/shard_map/ppermute | solution.py:475
  36.2 6.4 %collective-permute-start.7 = (bf16[64,1024]{1,0:T(8,128)(2,1)S(1)}, bf16[64,1024]{1,0:T(8,128)(2,1)S(1)}, u32[]{:S(2)}, u32[]{:S(2)}) collective-permute-start(bf16[64,1024]{1,0:T(8,128)(2,1)S(1)} %collective-permute-done.4.refs_1_), channel_id=1, source_target_pairs={{0,14},{2,0},{4,2},{6,4},{8,6},{10,8},{12,10},{14,12},{1,15},{3,1}... | collective-permute-start | bytes 393224 | tf_op jit(solution)/shard_map/ppermute | solution.py:475
  42.6 6.6 %collective-permute-start.9 = (bf16[64,1024]{1,0:T(8,128)(2,1)S(1)}, bf16[64,1024]{1,0:T(8,128)(2,1)S(1)}, u32[]{:S(2)}, u32[]{:S(2)}) collective-permute-start(bf16[64,1024]{1,0:T(8,128)(2,1)S(1)} %collective-permute-done.6.refs_0_), channel_id=1, source_target_pairs={{0,2},{2,4},{4,6},{6,8},{8,10},{10,12},{12,14},{14,0},{1,3},{3,5},... | collective-permute-start | bytes 393224 | tf_op jit(solution)/shard_map/ppermute | solution.py:475
  42.6 11.2 %collective-permute-start.10 = (bf16[64,1024]{1,0:T(8,128)(2,1)S(1)}, bf16[64,1024]{1,0:T(8,128)(2,1)S(1)}, u32[]{:S(2)}, u32[]{:S(2)}) collective-permute-start(bf16[64,1024]{1,0:T(8,128)(2,1)S(1)} %collective-permute-done.7.refs_1_), channel_id=1, source_target_pairs={{0,14},{2,0},{4,2},{6,4},{8,6},{10,8},{12,10},{14,12},{1,15},{3,1}... | collective-permute-start | bytes 393224 | tf_op jit(solution)/shard_map/ppermute | solution.py:475
  45.9 23.7 %collective-permute-start.5 = (bf16[128,1024]{1,0:T(8,128)(2,1)S(1)}, bf16[128,1024]{1,0:T(8,128)(2,1)S(1)}, u32[]{:S(2)}, u32[]{:S(2)}) collective-permute-start(bf16[128,1024]{1,0:T(8,128)(2,1)S(1)} %shard_map.29.refs_3_), channel_id=1, source_target_pairs={{0,16},{16,0},{1,17},{17,1},{2,18},{18,2},{3,19},{19,3},{4,20},{20... | collective-permute-start | bytes 786440 | tf_op jit(solution)/shard_map/ppermute | solution.py:475
  49.1 7.3 %collective-permute-start.12 = (bf16[64,1024]{1,0:T(8,128)(2,1)S(1)}, bf16[64,1024]{1,0:T(8,128)(2,1)S(1)}, u32[]{:S(2)}, u32[]{:S(2)}) collective-permute-start(bf16[64,1024]{1,0:T(8,128)(2,1)S(1)} %collective-permute-done.6.refs_0_), channel_id=1, source_target_pairs={{0,4},{2,6},{4,8},{6,10},{8,12},{10,14},{12,0},{14,2},{1,5},{3,7},... | collective-permute-start | bytes 393224 | tf_op jit(solution)/shard_map/ppermute | solution.py:475
  49.2 21.8 %collective-permute-start.8 = (bf16[128,1024]{1,0:T(8,128)(2,1)S(1)}, bf16[128,1024]{1,0:T(8,128)(2,1)S(1)}, u32[]{:S(2)}, u32[]{:S(2)}) collective-permute-start(bf16[128,1024]{1,0:T(8,128)(2,1)S(1)} %shard_map.30.refs_4_), channel_id=1, source_target_pairs={{0,16},{16,0},{1,17},{17,1},{2,18},{18,2},{3,19},{19,3},{4,20},{20... | collective-permute-start | bytes 786440 | tf_op jit(solution)/shard_map/ppermute | solution.py:475
  53.8 17.2 %collective-permute-start.11 = (bf16[128,1024]{1,0:T(8,128)(2,1)S(1)}, bf16[128,1024]{1,0:T(8,128)(2,1)S(1)}, u32[]{:S(2)}, u32[]{:S(2)}) collective-permute-start(bf16[128,1024]{1,0:T(8,128)(2,1)S(1)} %shard_map.31.refs_5_), channel_id=1, source_target_pairs={{0,16},{16,0},{1,17},{17,1},{2,18},{18,2},{3,19},{19,3},{4,20},{20... | collective-permute-start | bytes 786440 | tf_op jit(solution)/shard_map/ppermute | solution.py:475
  56.4 13.1 %collective-permute-start.2 = (bf16[64,1024]{1,0:T(8,128)(2,1)S(1)}, bf16[64,1024]{1,0:T(8,128)(2,1)S(1)}, u32[]{:S(2)}, u32[]{:S(2)}) collective-permute-start(bf16[64,1024]{1,0:T(8,128)(2,1)S(1)} %copy-done.1), channel_id=1, source_target_pairs={{0,16},{16,0},{1,17},{17,1},{2,18},{18,2},{3,19},{19,3},{4,20},{20... | collective-permute-start | bytes 393224 | tf_op jit(solution)/shard_map/ppermute | solution.py:475
  57.4 13.5 %collective-permute-start.13 = (bf16[64,1024]{1,0:T(8,128)(2,1)S(1)}, bf16[64,1024]{1,0:T(8,128)(2,1)S(1)}, u32[]{:S(2)}, u32[]{:S(2)}) collective-permute-start(bf16[64,1024]{1,0:T(8,128)(2,1)S(1)} %collective-permute-done.12.refs_6_), channel_id=1, source_target_pairs={{0,16},{16,0},{1,17},{17,1},{2,18},{18,2},{3,19},{19,3},{4,20},{20... | collective-permute-start | bytes 393224 | tf_op jit(solution)/shard_map/ppermute | solution.py:475
  194.4 6.9 %collective-permute-start.14 = (bf16[512,1024]{1,0:T(8,128)(2,1)S(1)}, bf16[512,1024]{1,0:T(8,128)(2,1)S(1)}, u32[]{:S(2)}, u32[]{:S(2)}) collective-permute-start(bf16[512,1024]{1,0:T(8,128)(2,1)S(1)} %get-tuple-element.38), channel_id=1, source_target_pairs={{0,1},{1,0},{2,3},{3,2},{4,5},{5,4},{6,7},{7,6},{8,9},{9,8},{10,11... | collective-permute-start | bytes 3145736 | tf_op jit(solution)/shard_map/ppermute | solution.py:475
  194.5 6.8 %collective-permute-start.15 = (f32[4,128]{1,0:T(4,128)S(1)}, f32[4,128]{1,0:T(4,128)S(1)}, u32[]{:S(2)}, u32[]{:S(2)}) collective-permute-start(f32[4,128]{1,0:T(4,128)S(1)} %get-tuple-element.39), channel_id=1, source_target_pairs={{0,1},{1,0},{2,3},{3,2},{4,5},{5,4},{6,7},{7,6},{8,9},{9,8},{10,11... | collective-permute-start | bytes 6152 | tf_op jit(solution)/shard_map/ppermute | solution.py:475
  195.0 6.3 %collective-permute-start.16 = (f32[4,128]{1,0:T(4,128)S(1)}, f32[4,128]{1,0:T(4,128)S(1)}, u32[]{:S(2)}, u32[]{:S(2)}) collective-permute-start(f32[4,128]{1,0:T(4,128)S(1)} %get-tuple-element.40), channel_id=1, source_target_pairs={{0,1},{1,0},{2,3},{3,2},{4,5},{5,4},{6,7},{7,6},{8,9},{9,8},{10,11... | collective-permute-start | bytes 6152 | tf_op jit(solution)/shard_map/ppermute | solution.py:475
where the time goes:
time: 224 us; the launch traced here: 223 us
  blocking collectives  110 us (49%)
  Pallas kernels  46.6 us (21%)
  waiting for transfers between devices  32.6 us (15%)
  starting transfers between devices  31.9 us (14%)
    all_to_all x9, blocking collectives, exchanged(): return lax.all_to_all(parts, axes, 0, 0, tiled=True)  110 us
    ppermute x17, starting transfers between devices, moved(): lax.ppermute(array, axis, [(k, (k + step) % size) for k in range(size)])  26.3 us
    ppermute x17, waiting for transfers between devices, moved(): lax.ppermute(array, axis, [(k, (k + step) % size) for k in range(size)])  20.5 us
    pallas_call x3, Pallas kernels, local(): parts = call(row_kernel, part, [wide], arrays=4)(terms, tile, parts, base)  13.1 us
    pallas_call x2, Pallas kernels, last(): call(functools.partial(last_kernel, mine, skip), (jax.ShapeDtypeStruct((c...  12.3 us
    all_to_all x1, waiting for transfers between devices, exchanged(): return lax.all_to_all(parts, axes, 0, 0, tiled=True)  12.1 us
    pallas_call x3, Pallas kernels, local(): call(column_kernel, part, [wide], arrays=4)(terms, tile, parts, base)  7.48 us
    all_to_all x1, starting transfers between devices, exchanged(): return lax.all_to_all(parts, axes, 0, 0, tiled=True)  5.6 us
  transfers between devices with their start and end apart: 18, of which 7 were waited for; matrix products, arithmetic and copies ran while one was open for 0% of the time, Pallas kernels for 5%

commit v1 on v0

--- a/solution.py
+++ b/solution.py
@@ -311,8 +311,8 @@
 
 
 def near_kernel(place_ref, *refs):
-    noise, own_ref, near = refs[:2], refs[2], refs[3:7]
-    block_ref, tile_ref, squares_ref, top_ref, sums_ref, line_ref, sem = refs[7:]
+    noise, own_ref, near = refs[:2], refs[2], refs[3:8]
+    block_ref, tile_ref, squares_ref, top_ref, sums_ref, line_ref, sem = refs[8:]
     y_hi, z, core = (place_ref[k] for k in range(2, 5))
     at = pl.multiple_of((y_hi * 8 + z) * 64, 64)
     fetch = pltpu.make_async_copy(own_ref, block_ref.at[pl.ds(at, 64), :], sem)
@@ -337,9 +337,9 @@
 
 
 def far_kernel(place_ref, *refs):
-    noise, far = refs[:2], refs[2:7]
-    squares_ref, top_ref, near_sums_ref, line_ref, _, _ = refs[7:13]
-    block_ref, tile_ref, out_ref, sums_ref = refs[13:]
+    noise, far = refs[:2], refs[2:8]
+    squares_ref, top_ref, near_sums_ref, line_ref, _, _ = refs[8:14]
+    block_ref, tile_ref, out_ref, sums_ref = refs[14:]
     y_hi, z, core = (place_ref[k] for k in range(2, 5))
     placed(far, block_ref, 1 - y_hi, z, PACKS)
     base = pl.multiple_of((1 - y_hi) * 512, 512)
@@ -445,7 +445,7 @@
                 wide_a * mine_ref[rows, here] + wide_b * other_ref[other_rows, here].astype(F32)
             ).astype(BF16)
     pieces = pieces_of(limit) + pieces_of(mass)
-    pieces = jnp.concatenate(pieces + [jnp.zeros_like(pieces[0])] * 2, axis=0)
+    pieces = jnp.concatenate(pieces, axis=0)
     for g in range(8):
         out_ref[g, count:, :] = pieces
 
@@ -453,7 +453,7 @@
 def groups_kernel(*refs):
     out_ref, start = refs[-1], 0
     for parts_ref in refs[:-1]:
-        count = parts_ref.shape[1] // 136 * 128
+        count = parts_ref.shape[1] // 134 * 128
         n = count // 128
         pieces = parts_ref[:, count:, :].astype(F32)
         limit = pieces[:, 0:n] + pieces[:, n : 2 * n] + pieces[:, 2 * n : 3 * n]
@@ -510,7 +510,9 @@
                 limit=2,
             )(*(near[back] for back in backs))
         )
-    far = [moved(pack, "y_hi", 1) for pack in packs]
+    across = moved(latents, "y_hi", 1)
+    far = [across, moved(across, "z", 1), moved(across, "z", -1)]
+    far += [moved(packs[k], "y_hi", 1) for k in range(3, len(packs))]
     noise_pair = moved(noise_draws, "y_lo", 1)
     spread = pl.pallas_call(
         spread_kernel,
@@ -532,11 +534,11 @@
         [pltpu.SemaphoreType.DMA],
         flops=1 << 30,
         scalars=1,
-        arrays=7,
+        arrays=8,
         kept=(3,),
     )(place, rows, other_rows, *packs)
     block, tile, parts = call(
-        far_kernel, (block_out, tile_out, part), [wide], 1 << 30, 1, 13, aliases={12: 0, 13: 1}
+        far_kernel, (block_out, tile_out, part), [wide], 1 << 30, 1, 14, aliases={13: 0, 14: 1}
     )(place, rows, other_rows, *far, squared, top, masses, peaks, block, tile)
     for sweep in range(ITERS):
         if sweep:
@@ -570,7 +572,7 @@
         own = last(True, skip, count, F32)
         message = call(
             functools.partial(cores_kernel, skip),
-            jax.ShapeDtypeStruct((8, count // 128 * 136, 128), BF16),
+            jax.ShapeDtypeStruct((8, count // 128 * 134, 128), BF16),
             arrays=6,
         )(*own, *other)
         messages.append(exchanged(message, OWNERS))
@@ -581,7 +583,7 @@
 
 
 OWN = (512,)
-PACKS = ((0,), (1, 7), (2, 6), (3, 5), (4,))
+PACKS = ((0,), (1,), (7,), (2, 6), (3, 5), (4,))
 
 
 def solution(mesh):

time: 224 us -> 219 us (0.978)
  waiting for transfers between devices: 32.6 us -> 27.1 us
    ppermute x17 -> x18, waiting for transfers between devices: 20.5 us -> 15 us  [moved(): lax.ppermute(array, axis, [(k, (k + step) % size) for k in range(size)])]
    ppermute x17 -> x18, starting transfers between devices: 26.3 us -> 27.3 us  [moved(): lax.ppermute(array, axis, [(k, (k + step) % size) for k in range(size)])]
  transfers between devices with their start and end apart: 18 -> 19, of which waited for: 7 -> 6; matrix products, arithmetic and copies ran while one was open for 0% -> 0% of each run, Pallas kernels for 5% -> 5%
where the time goes in v1:
time: 219 us; the launch traced here: 218 us
  blocking collectives  110 us (50%)
  Pallas kernels  46.6 us (21%)
  starting transfers between devices  32.9 us (15%)
  waiting for transfers between devices  27.1 us (12%)
    all_to_all x9, blocking collectives, exchanged(): return lax.all_to_all(parts, axes, 0, 0, tiled=True)  110 us
    ppermute x18, starting transfers between devices, moved(): lax.ppermute(array, axis, [(k, (k + step) % size) for k in range(size)])  27.3 us
    ppermute x18, waiting for transfers between devices, moved(): lax.ppermute(array, axis, [(k, (k + step) % size) for k in range(size)])  15 us
    pallas_call x3, Pallas kernels, local(): parts = call(row_kernel, part, [wide], arrays=4)(terms, tile, parts, base)  13.1 us
    pallas_call x2, Pallas kernels, last(): call(functools.partial(last_kernel, mine, skip), (jax.ShapeDtypeStruct((c...  12.3 us
    all_to_all x1, waiting for transfers between devices, exchanged(): return lax.all_to_all(parts, axes, 0, 0, tiled=True)  12.1 us
    pallas_call x3, Pallas kernels, local(): call(column_kernel, part, [wide], arrays=4)(terms, tile, parts, base)  7.48 us
    all_to_all x1, starting transfers between devices, exchanged(): return lax.all_to_all(parts, axes, 0, 0, tiled=True)  5.6 us
  transfers between devices with their start and end apart: 19, of which 6 were waited for; matrix products, arithmetic and copies ran while one was open for 0% of the time, Pallas kernels for 5%

profile of v1, /device:TPU:2, one launch (start us, length us, event | category | flops | bytes accessed | tf_op | source)
XLA Modules:
  0.0 217.9 jit_solution(16062833460548298094)
XLA Ops:
  1.6 3.9 %collective-permute-done.other_ref = bf16[512,128]{1,0:T(8,128)(2,1)S(1)} collective-permute-done((bf16[512,128]{1,0:T(8,128)(2,1)}, bf16[512,128]{1,0:T(8,128)(2,1)S(1)}, u32[]{:S(2)}, u32[]{:S(2)}) %collective-permute-start) | collective-permute-done | bytes 131104 | tf_op jit(solution)/shard_map/ppermute | solution.py:475
  7.5 5.6 %all-to-all-start = ((bf16[4,2,512,128]{3,2,1,0:T(8,128)(2,1)}), bf16[4,2,512,128]{3,2,1,0:T(8,128)(2,1)S(1)}, u32[]{:S(2)}, u32[]{:S(2)}) async-start(bf16[4,2,512,128]{3,2,1,0:T(8,128)(2,1)} %spread.1), calls=%async_computation | async-start | bytes 2097152 | tf_op jit(solution)/shard_map/all_to_all | solution.py:479
  13.1 12.1 %all-to-all-done.parts_ref = bf16[4,2,512,128]{3,2,1,0:T(8,128)(2,1)S(1)} async-done(((bf16[4,2,512,128]{3,2,1,0:T(8,128)(2,1)}), bf16[4,2,512,128]{3,2,1,0:T(8,128)(2,1)S(1)}, u32[]{:S(2)}, u32[]{:S(2)}) %all-to-all-start) | async-done | bytes 1048608 | tf_op jit(solution)/shard_map/all_to_all | solution.py:479
  28.2 4.0 %collective-permute-start.7 = (bf16[64,1024]{1,0:T(8,128)(2,1)S(1)}, bf16[64,1024]{1,0:T(8,128)(2,1)S(1)}, u32[]{:S(2)}, u32[]{:S(2)}) collective-permute-start(bf16[64,1024]{1,0:T(8,128)(2,1)S(1)} %copy-done.1), channel_id=1, source_target_pairs={{0,14},{2,0},{4,2},{6,4},{8,6},{10,8},{12,10},{14,12},{1,15},{3,1}... | collective-permute-start | bytes 393224 | tf_op jit(solution)/shard_map/ppermute | solution.py:475
  32.2 4.0 %collective-permute-done.5.refs_3_ = bf16[64,1024]{1,0:T(8,128)(2,1)S(1)} collective-permute-done((bf16[64,1024]{1,0:T(8,128)(2,1)S(1)}, bf16[64,1024]{1,0:T(8,128)(2,1)S(1)}, u32[]{:S(2)}, u32[]{:S(2)}) %collective-permute-start.5) | collective-permute-done | bytes 131104 | tf_op jit(solution)/shard_map/ppermute | solution.py:475
  36.2 3.2 %collective-permute-start.8 = (bf16[64,1024]{1,0:T(8,128)(2,1)S(1)}, bf16[64,1024]{1,0:T(8,128)(2,1)S(1)}, u32[]{:S(2)}, u32[]{:S(2)}) collective-permute-start(bf16[64,1024]{1,0:T(8,128)(2,1)S(1)} %collective-permute-done.7.refs_4_), channel_id=1, source_target_pairs={{0,14},{2,0},{4,2},{6,4},{8,6},{10,8},{12,10},{14,12},{1,15},{3,1}... | collective-permute-start | bytes 393224 | tf_op jit(solution)/shard_map/ppermute | solution.py:475
  39.4 3.2 %collective-permute-done.6.refs_0_ = bf16[64,1024]{1,0:T(8,128)(2,1)S(1)} collective-permute-done((bf16[64,1024]{1,0:T(8,128)(2,1)S(1)}, bf16[64,1024]{1,0:T(8,128)(2,1)S(1)}, u32[]{:S(2)}, u32[]{:S(2)}) %collective-permute-start.6) | collective-permute-done | bytes 131104 | tf_op jit(solution)/shard_map/ppermute | solution.py:475
  42.6 3.2 %collective-permute-start.11 = (bf16[64,1024]{1,0:T(8,128)(2,1)S(1)}, bf16[64,1024]{1,0:T(8,128)(2,1)S(1)}, u32[]{:S(2)}, u32[]{:S(2)}) collective-permute-start(bf16[64,1024]{1,0:T(8,128)(2,1)S(1)} %collective-permute-done.8.refs_1_), channel_id=1, source_target_pairs={{0,14},{2,0},{4,2},{6,4},{8,6},{10,8},{12,10},{14,12},{1,15},{3,1}... | collective-permute-start | bytes 393224 | tf_op jit(solution)/shard_map/ppermute | solution.py:475
  45.9 3.2 %collective-permute-start.2 = (bf16[64,1024]{1,0:T(8,128)(2,1)S(1)}, bf16[64,1024]{1,0:T(8,128)(2,1)S(1)}, u32[]{:S(2)}, u32[]{:S(2)}) collective-permute-start(bf16[64,1024]{1,0:T(8,128)(2,1)S(1)} %copy-done.1), channel_id=1, source_target_pairs={{0,16},{16,0},{1,17},{17,1},{2,18},{18,2},{3,19},{19,3},{4,20},{20... | collective-permute-start | bytes 393224 | tf_op jit(solution)/shard_map/ppermute | solution.py:475
  49.1 4.6 %collective-permute-start.9 = (bf16[128,1024]{1,0:T(8,128)(2,1)S(1)}, bf16[128,1024]{1,0:T(8,128)(2,1)S(1)}, u32[]{:S(2)}, u32[]{:S(2)}) collective-permute-start(bf16[128,1024]{1,0:T(8,128)(2,1)S(1)} %shard_map.29.refs_5_), channel_id=1, source_target_pairs={{0,16},{16,0},{1,17},{17,1},{2,18},{18,2},{3,19},{19,3},{4,20},{20... | collective-permute-start | bytes 786440 | tf_op jit(solution)/shard_map/ppermute | solution.py:475
  56.3 3.0 %collective-permute-start.14 = (bf16[64,1024]{1,0:T(8,128)(2,1)S(1)}, bf16[64,1024]{1,0:T(8,128)(2,1)S(1)}, u32[]{:S(2)}, u32[]{:S(2)}) collective-permute-start(bf16[64,1024]{1,0:T(8,128)(2,1)S(1)} %collective-permute-done.13.refs_7_), channel_id=1, source_target_pairs={{0,16},{16,0},{1,17},{17,1},{2,18},{18,2},{3,19},{19,3},{4,20},{20... | collective-permute-start | bytes 393224 | tf_op jit(solution)/shard_map/ppermute | solution.py:475
  59.4 4.1 %shard_map.31 = (bf16[1024,1024]{1,0:T(8,128)(2,1)S(1)}, f32[1024,1024]{1,0:T(8,128)S(1)}, f32[1024,128]{1,0:T(8,128)S(1)}, f32[1024,128]{1,0:T(8,128)S(1)}, f32...) custom-call(s32[5]{0:T(128)S(1)} %stack.23.place_ref, bf16[512,1024]{1,0:T(8,128)(2,1)S(1)} %shard_map.28.refs_0_, ...), custom_call_target="tpu_custom_call" | custom-call | flops 1073741824 | bytes 4194304 | tf_op jit(solution)/shard_map/pallas_call | solution.py:531
  63.5 2.9 %collective-permute-done.14.refs_7_ = bf16[64,1024]{1,0:T(8,128)(2,1)S(1)} collective-permute-done((bf16[64,1024]{1,0:T(8,128)(2,1)S(1)}, bf16[64,1024]{1,0:T(8,128)(2,1)S(1)}, u32[]{:S(2)}, u32[]{:S(2)}) %collective-permute-start.14) | collective-permute-done | bytes 131104 | tf_op jit(solution)/shard_map/ppermute | solution.py:475
  66.4 3.0 %shard_map.32 = (bf16[1024,1024]{1,0:T(8,128)(2,1)S(1)}, f32[1024,1024]{1,0:T(8,128)S(1)}, f32[16,8,128]{2,1,0:T(8,128)S(1)}) custom-call(s32[5]{0:T(128)S(1)} %stack.23.place_ref, bf16[512,1024]{1,0:T(8,128)(2,1)S(1)} %shard_map.28.refs_0_, bf16[512,1024]{1,0:T(8,128)(2,1)S(1)} %collective-permute-done.1.refs_1_, ...), custom_call_target="tpu_custom_call", output_to_operand_aliasing={{0}: (13, {}), {1}: (14, {})} | custom-call | flops 1073741824 | bytes 4194304 | tf_op jit(solution)/shard_map/pallas_call | solution.py:540
  69.4 9.3 %all_to_all.50.parts_ref = f32[16,8,128]{2,1,0:T(8,128)S(1)} all-to-all(f32[16,8,128]{2,1,0:T(8,128)S(1)} %get-tuple-element.30), channel_id=1, replica_groups=mesh['y_lo'=2,'x'=4,'y_hi'=2,'z'=8,'core'=2] {'y_lo','x','core'}, dimensions={0} | all-to-all | bytes 131072 | tf_op jit(solution)/shard_map/all_to_all | solution.py:479
  78.7 2.9 %shard_map.33 = (f32[16,8,128]{2,1,0:T(8,128)S(1)}, f32[8,128]{1,0:T(8,128)S(1)}, f32[1024,1024]{1,0:T(8,128)S(1)}) custom-call(f32[1024,1024]{1,0:T(8,128)S(1)} %get-tuple-element.29.tile_ref, f32[16,8,128]{2,1,0:T(8,128)S(1)} %all_to_all.50.parts_ref), custom_call_target="tpu_custom_call" | custom-call | bytes 4194304 | tf_op jit(solution)/shard_map/pallas_call | solution.py:550
  81.6 17.0 %all_to_all.51.parts_ref = f32[16,8,128]{2,1,0:T(8,128)S(1)} all-to-all(f32[16,8,128]{2,1,0:T(8,128)S(1)} %get-tuple-element.32), channel_id=1, replica_groups=mesh['y_lo'=2,'x'=4,'y_hi'=2,'z'=8,'core'=2] {'y_hi','z'}, dimensions={0} | all-to-all | bytes 131072 | tf_op jit(solution)/shard_map/all_to_all | solution.py:479
  98.6 4.4 %shard_map.34 = f32[16,8,128]{2,1,0:T(8,128)S(1)} custom-call(f32[1024,1024]{1,0:T(8,128)S(1)} %get-tuple-element.31.terms_ref, f32[1024,1024]{1,0:T(8,128)S(1)} %get-tuple-element.29.tile_ref, f32[16,8,128]{2,1,0:T(8,128)S(1)} %all_to_all.51.parts_ref, f32[8,128]{1,0:T(8,128)S(1)} %get-tuple-element.33.base_ref), custom_call_target="tpu_custom_call" | custom-call | bytes 4194304 | tf_op jit(solution)/shard_map/pallas_call | solution.py:545
  103.0 8.7 %all_to_all.52.parts_ref = f32[16,8,128]{2,1,0:T(8,128)S(1)} all-to-all(f32[16,8,128]{2,1,0:T(8,128)S(1)} %shard_map.34), channel_id=1, replica_groups=mesh['y_lo'=2,'x'=4,'y_hi'=2,'z'=8,'core'=2] {'y_lo','x','core'}, dimensions={0} | all-to-all | bytes 131072 | tf_op jit(solution)/shard_map/all_to_all | solution.py:479
  111.7 2.5 %shard_map.35 = f32[16,8,128]{2,1,0:T(8,128)S(1)} custom-call(f32[1024,1024]{1,0:T(8,128)S(1)} %get-tuple-element.31.terms_ref, f32[1024,1024]{1,0:T(8,128)S(1)} %get-tuple-element.29.tile_ref, f32[16,8,128]{2,1,0:T(8,128)S(1)} %all_to_all.52.parts_ref, f32[8,128]{1,0:T(8,128)S(1)} %get-tuple-element.33.base_ref), custom_call_target="tpu_custom_call" | custom-call | bytes 4194304 | tf_op jit(solution)/shard_map/pallas_call | solution.py:548
  114.2 12.6 %all_to_all.53.parts_ref = f32[16,8,128]{2,1,0:T(8,128)S(1)} all-to-all(f32[16,8,128]{2,1,0:T(8,128)S(1)} %shard_map.35), channel_id=1, replica_groups=mesh['y_lo'=2,'x'=4,'y_hi'=2,'z'=8,'core'=2] {'y_hi','z'}, dimensions={0} | all-to-all | bytes 131072 | tf_op jit(solution)/shard_map/all_to_all | solution.py:479
  126.8 4.4 %shard_map.36 = f32[16,8,128]{2,1,0:T(8,128)S(1)} custom-call(f32[1024,1024]{1,0:T(8,128)S(1)} %get-tuple-element.31.terms_ref, f32[1024,1024]{1,0:T(8,128)S(1)} %get-tuple-element.29.tile_ref, f32[16,8,128]{2,1,0:T(8,128)S(1)} %all_to_all.53.parts_ref, f32[8,128]{1,0:T(8,128)S(1)} %get-tuple-element.33.base_ref), custom_call_target="tpu_custom_call" | custom-call | bytes 4194304 | tf_op jit(solution)/shard_map/pallas_call | solution.py:545
  131.2 8.7 %all_to_all.54.parts_ref = f32[16,8,128]{2,1,0:T(8,128)S(1)} all-to-all(f32[16,8,128]{2,1,0:T(8,128)S(1)} %shard_map.36), channel_id=1, replica_groups=mesh['y_lo'=2,'x'=4,'y_hi'=2,'z'=8,'core'=2] {'y_lo','x','core'}, dimensions={0} | all-to-all | bytes 131072 | tf_op jit(solution)/shard_map/all_to_all | solution.py:479
  139.9 2.5 %shard_map.37 = f32[16,8,128]{2,1,0:T(8,128)S(1)} custom-call(f32[1024,1024]{1,0:T(8,128)S(1)} %get-tuple-element.31.terms_ref, f32[1024,1024]{1,0:T(8,128)S(1)} %get-tuple-element.29.tile_ref, f32[16,8,128]{2,1,0:T(8,128)S(1)} %all_to_all.54.parts_ref, f32[8,128]{1,0:T(8,128)S(1)} %get-tuple-element.33.base_ref), custom_call_target="tpu_custom_call" | custom-call | bytes 4194304 | tf_op jit(solution)/shard_map/pallas_call | solution.py:548
  142.4 12.9 %all_to_all.55.parts_ref = f32[16,8,128]{2,1,0:T(8,128)S(1)} all-to-all(f32[16,8,128]{2,1,0:T(8,128)S(1)} %shard_map.37), channel_id=1, replica_groups=mesh['y_lo'=2,'x'=4,'y_hi'=2,'z'=8,'core'=2] {'y_hi','z'}, dimensions={0} | all-to-all | bytes 131072 | tf_op jit(solution)/shard_map/all_to_all | solution.py:479
  155.3 4.4 %shard_map.38 = f32[16,8,128]{2,1,0:T(8,128)S(1)} custom-call(f32[1024,1024]{1,0:T(8,128)S(1)} %get-tuple-element.31.terms_ref, f32[1024,1024]{1,0:T(8,128)S(1)} %get-tuple-element.29.tile_ref, f32[16,8,128]{2,1,0:T(8,128)S(1)} %all_to_all.55.parts_ref, f32[8,128]{1,0:T(8,128)S(1)} %get-tuple-element.33.base_ref), custom_call_target="tpu_custom_call" | custom-call | bytes 4194304 | tf_op jit(solution)/shard_map/pallas_call | solution.py:545
  159.6 8.7 %all_to_all.56.parts_ref = f32[16,8,128]{2,1,0:T(8,128)S(1)} all-to-all(f32[16,8,128]{2,1,0:T(8,128)S(1)} %shard_map.38), channel_id=1, replica_groups=mesh['y_lo'=2,'x'=4,'y_hi'=2,'z'=8,'core'=2] {'y_lo','x','core'}, dimensions={0} | all-to-all | bytes 131072 | tf_op jit(solution)/shard_map/all_to_all | solution.py:479
  168.3 2.5 %shard_map.39 = f32[16,8,128]{2,1,0:T(8,128)S(1)} custom-call(f32[1024,1024]{1,0:T(8,128)S(1)} %get-tuple-element.31.terms_ref, f32[1024,1024]{1,0:T(8,128)S(1)} %get-tuple-element.29.tile_ref, f32[16,8,128]{2,1,0:T(8,128)S(1)} %all_to_all.56.parts_ref, f32[8,128]{1,0:T(8,128)S(1)} %get-tuple-element.33.base_ref), custom_call_target="tpu_custom_call" | custom-call | bytes 4194304 | tf_op jit(solution)/shard_map/pallas_call | solution.py:548
  170.8 12.6 %all_to_all.57.parts_ref = f32[16,8,128]{2,1,0:T(8,128)S(1)} all-to-all(f32[16,8,128]{2,1,0:T(8,128)S(1)} %shard_map.39), channel_id=1, replica_groups=mesh['y_lo'=2,'x'=4,'y_hi'=2,'z'=8,'core'=2] {'y_hi','z'}, dimensions={0} | all-to-all | bytes 131072 | tf_op jit(solution)/shard_map/all_to_all | solution.py:479
  183.5 6.2 %shard_map.41 = (bf16[512,1024]{1,0:T(8,128)(2,1)S(1)}, f32[4,128]{1,0:T(4,128)S(1)}, f32[4,128]{1,0:T(4,128)S(1)}) custom-call(s32[1]{0:T(128)} %bitcast.core_ref, f32[1024,1024]{1,0:T(8,128)S(1)} %get-tuple-element.31.terms_ref, f32[1024,1024]{1,0:T(8,128)S(1)} %get-tuple-element.29.tile_ref, f32[16,8,128]{2,1,0:T(8,128)S(1)} %all_to_all.57.parts_ref, ...), custom_call_target="tpu_custom_call" | custom-call | flops 1073741824 | bytes 4194304 | tf_op jit(solution)/shard_map/pallas_call | solution.py:559
  190.4 6.2 %shard_map.40 = (f32[512,1024]{1,0:T(8,128)S(1)}, f32[4,128]{1,0:T(4,128)S(1)}, f32[4,128]{1,0:T(4,128)S(1)}) custom-call(s32[1]{0:T(128)} %bitcast.core_ref, f32[1024,1024]{1,0:T(8,128)S(1)} %get-tuple-element.31.terms_ref, f32[1024,1024]{1,0:T(8,128)S(1)} %get-tuple-element.29.tile_ref, f32[16,8,128]{2,1,0:T(8,128)S(1)} %all_to_all.57.parts_ref, ...), custom_call_target="tpu_custom_call" | custom-call | flops 1073741824 | bytes 4194304 | tf_op jit(solution)/shard_map/pallas_call | solution.py:559
  197.0 19.6 %all_to_all.58.refs_0_ = bf16[8,536,128]{2,1,0:T(8,128)(2,1)S(1)} all-to-all(bf16[8,536,128]{2,1,0:T(8,128)(2,1)S(1)} %shard_map.42), channel_id=1, replica_groups=mesh['y_lo'=2,'x'=4,'y_hi'=2,'z'=8,'core'=2] {'x','y_lo'}, dimensions={0} | all-to-all | bytes 2195456 | tf_op jit(solution)/shard_map/all_to_all | solution.py:479
  (37 shorter events, 11.7 us)
Async XLA Ops:
  0.0 5.4 %collective-permute-start = (bf16[512,128]{1,0:T(8,128)(2,1)}, bf16[512,128]{1,0:T(8,128)(2,1)S(1)}, u32[]{:S(2)}, u32[]{:S(2)}) collective-permute-start(bf16[512,128]{1,0:T(8,128)(2,1)} %noise_ref.1), channel_id=1, source_target_pairs={{0,128},{128,0},{1,129},{129,1},{2,130},{130,2},{3,131},{131,3},{4... | collective-permute-start | bytes 393224 | tf_op jit(solution)/shard_map/ppermute | solution.py:475
  5.4 0.9 copy-start
  7.4 18.7 %copy-start.1 = (bf16[64,1024]{1,0:T(8,128)(2,1)S(1)}, bf16[64,1024]{1,0:T(8,128)(2,1)}, u32[]{:S(2)}) copy-start(bf16[64,1024]{1,0:T(8,128)(2,1)} %refs_2_.1) | copy-start | bytes 393220
  7.5 17.8 %all-to-all-start = ((bf16[4,2,512,128]{3,2,1,0:T(8,128)(2,1)}), bf16[4,2,512,128]{3,2,1,0:T(8,128)(2,1)S(1)}, u32[]{:S(2)}, u32[]{:S(2)}) async-start(bf16[4,2,512,128]{3,2,1,0:T(8,128)(2,1)} %spread.1), calls=%async_computation | async-start | bytes 2097152 | tf_op jit(solution)/shard_map/all_to_all | solution.py:479
  26.1 30.3 %collective-permute-start.1 = (bf16[512,1024]{1,0:T(8,128)(2,1)S(1)}, bf16[512,1024]{1,0:T(8,128)(2,1)S(1)}, u32[]{:S(2)}, u32[]{:S(2)}) collective-permute-start(bf16[512,1024]{1,0:T(8,128)(2,1)S(1)} %shard_map.28.refs_0_), channel_id=1, source_target_pairs={{0,1},{1,0},{2,3},{3,2},{4,5},{5,4},{6,7},{7,6},{8,9},{9,8},{10,11... | collective-permute-start | bytes 3145736 | tf_op jit(solution)/shard_map/ppermute | solution.py:475
  26.2 10.0 %collective-permute-start.5 = (bf16[64,1024]{1,0:T(8,128)(2,1)S(1)}, bf16[64,1024]{1,0:T(8,128)(2,1)S(1)}, u32[]{:S(2)}, u32[]{:S(2)}) collective-permute-start(bf16[64,1024]{1,0:T(8,128)(2,1)S(1)} %copy-done.1), channel_id=1, source_target_pairs={{0,2},{2,4},{4,6},{6,8},{8,10},{10,12},{12,14},{14,0},{1,3},{3,5},... | collective-permute-start | bytes 393224 | tf_op jit(solution)/shard_map/ppermute | solution.py:475
  28.2 8.0 %collective-permute-start.7 = (bf16[64,1024]{1,0:T(8,128)(2,1)S(1)}, bf16[64,1024]{1,0:T(8,128)(2,1)S(1)}, u32[]{:S(2)}, u32[]{:S(2)}) collective-permute-start(bf16[64,1024]{1,0:T(8,128)(2,1)S(1)} %copy-done.1), channel_id=1, source_target_pairs={{0,14},{2,0},{4,2},{6,4},{8,6},{10,8},{12,10},{14,12},{1,15},{3,1}... | collective-permute-start | bytes 393224 | tf_op jit(solution)/shard_map/ppermute | solution.py:475
  36.2 6.4 %collective-permute-start.6 = (bf16[64,1024]{1,0:T(8,128)(2,1)S(1)}, bf16[64,1024]{1,0:T(8,128)(2,1)S(1)}, u32[]{:S(2)}, u32[]{:S(2)}) collective-permute-start(bf16[64,1024]{1,0:T(8,128)(2,1)S(1)} %collective-permute-done.5.refs_3_), channel_id=1, source_target_pairs={{0,2},{2,4},{4,6},{6,8},{8,10},{10,12},{12,14},{14,0},{1,3},{3,5},... | collective-permute-start | bytes 393224 | tf_op jit(solution)/shard_map/ppermute | solution.py:475
  36.2 6.4 %collective-permute-start.8 = (bf16[64,1024]{1,0:T(8,128)(2,1)S(1)}, bf16[64,1024]{1,0:T(8,128)(2,1)S(1)}, u32[]{:S(2)}, u32[]{:S(2)}) collective-permute-start(bf16[64,1024]{1,0:T(8,128)(2,1)S(1)} %collective-permute-done.7.refs_4_), channel_id=1, source_target_pairs={{0,14},{2,0},{4,2},{6,4},{8,6},{10,8},{12,10},{14,12},{1,15},{3,1}... | collective-permute-start | bytes 393224 | tf_op jit(solution)/shard_map/ppermute | solution.py:475
  42.6 6.5 %collective-permute-start.10 = (bf16[64,1024]{1,0:T(8,128)(2,1)S(1)}, bf16[64,1024]{1,0:T(8,128)(2,1)S(1)}, u32[]{:S(2)}, u32[]{:S(2)}) collective-permute-start(bf16[64,1024]{1,0:T(8,128)(2,1)S(1)} %collective-permute-done.6.refs_0_), channel_id=1, source_target_pairs={{0,2},{2,4},{4,6},{6,8},{8,10},{10,12},{12,14},{14,0},{1,3},{3,5},... | collective-permute-start | bytes 393224 | tf_op jit(solution)/shard_map/ppermute | solution.py:475
  42.6 11.1 %collective-permute-start.11 = (bf16[64,1024]{1,0:T(8,128)(2,1)S(1)}, bf16[64,1024]{1,0:T(8,128)(2,1)S(1)}, u32[]{:S(2)}, u32[]{:S(2)}) collective-permute-start(bf16[64,1024]{1,0:T(8,128)(2,1)S(1)} %collective-permute-done.8.refs_1_), channel_id=1, source_target_pairs={{0,14},{2,0},{4,2},{6,4},{8,6},{10,8},{12,10},{14,12},{1,15},{3,1}... | collective-permute-start | bytes 393224 | tf_op jit(solution)/shard_map/ppermute | solution.py:475
  45.9 7.9 %collective-permute-start.2 = (bf16[64,1024]{1,0:T(8,128)(2,1)S(1)}, bf16[64,1024]{1,0:T(8,128)(2,1)S(1)}, u32[]{:S(2)}, u32[]{:S(2)}) collective-permute-start(bf16[64,1024]{1,0:T(8,128)(2,1)S(1)} %copy-done.1), channel_id=1, source_target_pairs={{0,16},{16,0},{1,17},{17,1},{2,18},{18,2},{3,19},{19,3},{4,20},{20... | collective-permute-start | bytes 393224 | tf_op jit(solution)/shard_map/ppermute | solution.py:475
  49.1 7.3 %collective-permute-start.13 = (bf16[64,1024]{1,0:T(8,128)(2,1)S(1)}, bf16[64,1024]{1,0:T(8,128)(2,1)S(1)}, u32[]{:S(2)}, u32[]{:S(2)}) collective-permute-start(bf16[64,1024]{1,0:T(8,128)(2,1)S(1)} %collective-permute-done.6.refs_0_), channel_id=1, source_target_pairs={{0,4},{2,6},{4,8},{6,10},{8,12},{10,14},{12,0},{14,2},{1,5},{3,7},... | collective-permute-start | bytes 393224 | tf_op jit(solution)/shard_map/ppermute | solution.py:475
  49.1 17.3 %collective-permute-start.9 = (bf16[128,1024]{1,0:T(8,128)(2,1)S(1)}, bf16[128,1024]{1,0:T(8,128)(2,1)S(1)}, u32[]{:S(2)}, u32[]{:S(2)}) collective-permute-start(bf16[128,1024]{1,0:T(8,128)(2,1)S(1)} %shard_map.29.refs_5_), channel_id=1, source_target_pairs={{0,16},{16,0},{1,17},{17,1},{2,18},{18,2},{3,19},{19,3},{4,20},{20... | collective-permute-start | bytes 786440 | tf_op jit(solution)/shard_map/ppermute | solution.py:475
  53.7 12.7 %collective-permute-start.12 = (bf16[128,1024]{1,0:T(8,128)(2,1)S(1)}, bf16[128,1024]{1,0:T(8,128)(2,1)S(1)}, u32[]{:S(2)}, u32[]{:S(2)}) collective-permute-start(bf16[128,1024]{1,0:T(8,128)(2,1)S(1)} %shard_map.30.refs_6_), channel_id=1, source_target_pairs={{0,16},{16,0},{1,17},{17,1},{2,18},{18,2},{3,19},{19,3},{4,20},{20... | collective-permute-start | bytes 786440 | tf_op jit(solution)/shard_map/ppermute | solution.py:475
  53.8 9.6 %collective-permute-start.4 = (bf16[64,1024]{1,0:T(8,128)(2,1)S(1)}, bf16[64,1024]{1,0:T(8,128)(2,1)S(1)}, u32[]{:S(2)}, u32[]{:S(2)}) collective-permute-start(bf16[64,1024]{1,0:T(8,128)(2,1)S(1)} %collective-permute-done.2.refs_2_), channel_id=1, source_target_pairs={{0,14},{2,0},{4,2},{6,4},{8,6},{10,8},{12,10},{14,12},{1,15},{3,1}... | collective-permute-start | bytes 393224 | tf_op jit(solution)/shard_map/ppermute | solution.py:475
  56.3 7.1 %collective-permute-start.3 = (bf16[64,1024]{1,0:T(8,128)(2,1)S(1)}, bf16[64,1024]{1,0:T(8,128)(2,1)S(1)}, u32[]{:S(2)}, u32[]{:S(2)}) collective-permute-start(bf16[64,1024]{1,0:T(8,128)(2,1)S(1)} %collective-permute-done.2.refs_2_), channel_id=1, source_target_pairs={{0,2},{2,4},{4,6},{6,8},{8,10},{10,12},{12,14},{14,0},{1,3},{3,5},... | collective-permute-start | bytes 393224 | tf_op jit(solution)/shard_map/ppermute | solution.py:475
  56.3 10.0 %collective-permute-start.14 = (bf16[64,1024]{1,0:T(8,128)(2,1)S(1)}, bf16[64,1024]{1,0:T(8,128)(2,1)S(1)}, u32[]{:S(2)}, u32[]{:S(2)}) collective-permute-start(bf16[64,1024]{1,0:T(8,128)(2,1)S(1)} %collective-permute-done.13.refs_7_), channel_id=1, source_target_pairs={{0,16},{16,0},{1,17},{17,1},{2,18},{18,2},{3,19},{19,3},{4,20},{20... | collective-permute-start | bytes 393224 | tf_op jit(solution)/shard_map/ppermute | solution.py:475
  189.7 6.9 %collective-permute-start.15 = (bf16[512,1024]{1,0:T(8,128)(2,1)S(1)}, bf16[512,1024]{1,0:T(8,128)(2,1)S(1)}, u32[]{:S(2)}, u32[]{:S(2)}) collective-permute-start(bf16[512,1024]{1,0:T(8,128)(2,1)S(1)} %get-tuple-element.38), channel_id=1, source_target_pairs={{0,1},{1,0},{2,3},{3,2},{4,5},{5,4},{6,7},{7,6},{8,9},{9,8},{10,11... | collective-permute-start | bytes 3145736 | tf_op jit(solution)/shard_map/ppermute | solution.py:475
  189.8 6.8 %collective-permute-start.16 = (f32[4,128]{1,0:T(4,128)S(1)}, f32[4,128]{1,0:T(4,128)S(1)}, u32[]{:S(2)}, u32[]{:S(2)}) collective-permute-start(f32[4,128]{1,0:T(4,128)S(1)} %get-tuple-element.39), channel_id=1, source_target_pairs={{0,1},{1,0},{2,3},{3,2},{4,5},{5,4},{6,7},{7,6},{8,9},{9,8},{10,11... | collective-permute-start | bytes 6152 | tf_op jit(solution)/shard_map/ppermute | solution.py:475
  190.3 6.3 %collective-permute-start.17 = (f32[4,128]{1,0:T(4,128)S(1)}, f32[4,128]{1,0:T(4,128)S(1)}, u32[]{:S(2)}, u32[]{:S(2)}) collective-permute-start(f32[4,128]{1,0:T(4,128)S(1)} %get-tuple-element.40), channel_id=1, source_target_pairs={{0,1},{1,0},{2,3},{3,2},{4,5},{5,4},{6,7},{7,6},{8,9},{9,8},{10,11... | collective-permute-start | bytes 6152 | tf_op jit(solution)/shard_map/ppermute | solution.py:475

commit v2 on v0

--- a/solution.py
+++ b/solution.py
@@ -1,4 +1,3 @@
-import functools
 import math
 
 import jax
@@ -228,13 +227,6 @@
         column_part(tile_ref, dual, out_ref, wide_ref)
 
 
-def noise_kernel(place_ref, parts_ref, rows_ref):
-    for k in range(4):
-        for other in range(2):
-            at = jnp.bitwise_xor(place_ref[0], other) * 4 + k
-            rows_ref[:, pl.ds(pl.multiple_of(at * 128, 128), 128)] = parts_ref[k, other]
-
-
 def spread_kernel(noise_ref, other_ref, out_ref, sems):
     copies = [
         pltpu.make_async_copy(ref, out_ref.at[k, j], sems.at[k, j])
@@ -260,31 +252,25 @@
     return jnp.sum(total, axis=1, keepdims=True)
 
 
-def costs(noise, starts, block_ref, tile_ref, squares_ref, base, use):
+def costs(rows_ref, block_ref, tile_ref, squares_ref, base, use):
     eye = diagonal()
 
     @pl.loop(0, 2)
     def _(at):
         cols = pl.ds(pl.multiple_of(base + at * 256, 256), 256)
         latent_sq = squares(block_ref, cols)
-        for start, ref in zip(starts, noise):
-            cross = lax.dot_general(
-                ref[...], block_ref[cols, :], (((1,), (1,)), ((), ())), preferred_element_type=F32
-            )
-            rows, pair = pl.ds(start, 512), []
-            for k in range(2):
-                spread = jnp.broadcast_to(latent_sq[k * 128 : (k + 1) * 128], (128, 128))
-                line = jnp.sum(jnp.where(eye, spread, 0.0), axis=0, keepdims=True)
-                line = jnp.broadcast_to(line, (512, 128))
-                cost = squares_ref[rows, :] + line - 2.0 * cross[:, k * 128 : (k + 1) * 128]
-                cost = cost * (-SCALE / FEATURES)
-                tile_ref[rows, pl.ds(pl.multiple_of(base + at * 256 + k * 128, 128), 128)] = cost
-                pair.append(cost)
-            use(at, rows, pair)
-
-
-def halves(core):
-    return [pl.multiple_of(jnp.bitwise_xor(core, half) * 512, 512) for half in range(2)]
+        cross = lax.dot_general(
+            rows_ref[...], block_ref[cols, :], (((1,), (1,)), ((), ())), preferred_element_type=F32
+        )
+        pair = []
+        for k in range(2):
+            spread = jnp.broadcast_to(latent_sq[k * 128 : (k + 1) * 128], (128, 128))
+            line = jnp.sum(jnp.where(eye, spread, 0.0), axis=0, keepdims=True)
+            cost = squares_ref[...] + line - 2.0 * cross[:, k * 128 : (k + 1) * 128]
+            cost = cost * (-SCALE / FEATURES)
+            tile_ref[:, pl.ds(pl.multiple_of(base + at * 256 + k * 128, 128), 128)] = cost
+            pair.append(cost)
+        use(at, pair)
 
 
 def placed(packs, block_ref, group, z, orders):
@@ -311,45 +297,52 @@
 
 
 def near_kernel(place_ref, *refs):
-    noise, own_ref, near = refs[:2], refs[2], refs[3:7]
-    block_ref, tile_ref, squares_ref, top_ref, sums_ref, line_ref, sem = refs[7:]
-    y_hi, z, core = (place_ref[k] for k in range(2, 5))
-    at = pl.multiple_of((y_hi * 8 + z) * 64, 64)
-    fetch = pltpu.make_async_copy(own_ref, block_ref.at[pl.ds(at, 64), :], sem)
-    fetch.start()
+    noise, singles, near = refs[:2], refs[2:3], refs[3:7]
+    rows_ref, block_ref, tile_ref, squares_ref, top_ref, sums_ref, line_ref, sems = refs[7:]
+    y_lo, y_hi, z, core = (place_ref[k] for k in (0, 2, 3, 4))
+    fetches = []
+    for k, (single, backs) in enumerate(zip(singles, PACKS)):
+        at = y_hi * 8 + jnp.bitwise_and(z - backs[0] + 8, 7)
+        home = block_ref.at[pl.ds(pl.multiple_of(at * 64, 64), 64), :]
+        fetches.append(pltpu.make_async_copy(single, home, sems.at[k]))
+        fetches[-1].start()
+    for half, ref in enumerate(noise):
+        rows = pl.ds(pl.multiple_of(jnp.bitwise_xor(core, half) * 512, 512), 512)
+        for k in range(4):
+            for other in range(2):
+                at = jnp.bitwise_xor(y_lo, other) * 4 + k
+                rows_ref[rows, pl.ds(pl.multiple_of(at * 128, 128), 128)] = ref[k, other]
     placed(near, block_ref, y_hi, z, PACKS[1:])
-    starts = halves(core)
-    for start, ref in zip(starts, noise):
-        for k in range(4):
-            squares_ref[pl.ds(start + k * 128, 128), :] = jnp.broadcast_to(
-                squares(ref, slice(k * 128, (k + 1) * 128)), (128, 128)
-            )
-    fetch.wait()
+    for k in range(8):
+        rows = slice(k * 128, (k + 1) * 128)
+        squares_ref[rows, :] = jnp.broadcast_to(squares(rows_ref, rows), (128, 128))
+    for fetch in fetches:
+        fetch.wait()
     base = pl.multiple_of(y_hi * 512, 512)
 
-    def use(at, rows, pair):
+    def use(at, pair):
         top = jnp.maximum(*pair)
-        top_ref[rows, :] = jnp.maximum(jnp.where(at == 0, top, top_ref[rows, :]), top)
-
-    costs(noise, starts, block_ref, tile_ref, squares_ref, base, use)
+        top_ref[...] = jnp.maximum(jnp.where(at == 0, top, top_ref[...]), top)
+
+    costs(rows_ref, block_ref, tile_ref, squares_ref, base, use)
     first_masses(tile_ref, base, top_ref, sums_ref)
     line_ref[...] = to_lanes(top_ref[...], diagonal())
 
 
-def far_kernel(place_ref, *refs):
-    noise, far = refs[:2], refs[2:7]
-    squares_ref, top_ref, near_sums_ref, line_ref, _, _ = refs[7:13]
-    block_ref, tile_ref, out_ref, sums_ref = refs[13:]
-    y_hi, z, core = (place_ref[k] for k in range(2, 5))
+def far_kernel(place_ref, rows_ref, *refs):
+    far = refs[:5]
+    squares_ref, top_ref, near_sums_ref, line_ref, _, _ = refs[5:11]
+    block_ref, tile_ref, out_ref, sums_ref = refs[11:]
+    y_hi, z = place_ref[2], place_ref[3]
     placed(far, block_ref, 1 - y_hi, z, PACKS)
     base = pl.multiple_of((1 - y_hi) * 512, 512)
     sums_ref[...] = near_sums_ref[...]
 
-    def use(at, rows, pair):
-        top = top_ref[rows, :]
-        sums_ref[rows, :] = sums_ref[rows, :] + (jnp.exp2(pair[0] - top) + jnp.exp2(pair[1] - top))
-
-    costs(noise, halves(core), block_ref, tile_ref, squares_ref, base, use)
+    def use(at, pair):
+        top = top_ref[...]
+        sums_ref[...] = sums_ref[...] + (jnp.exp2(pair[0] - top) + jnp.exp2(pair[1] - top))
+
+    costs(rows_ref, block_ref, tile_ref, squares_ref, base, use)
     largest = jnp.max(sums_ref[...])
     lse = line_ref[...] + jnp.log2(lane_sums(sums_ref[...]))
     out_ref[...] = jnp.broadcast_to(lse[None], out_ref.shape)
@@ -359,63 +352,79 @@
         row_part(tile_ref, jnp.zeros((8, 128), F32), out_ref, sums_ref)
 
 
-def last_kernel(
-    mine, skip, core_ref, terms_ref, tile_ref, parts_ref, base_ref, block_ref,
-    out_ref, limit_ref, mass_ref, wide_ref, sums_ref, weights_ref,
+def away_kernel(
+    core_ref, terms_ref, tile_ref, parts_ref, base_ref, block_ref,
+    out_ref, limit_ref, mass_ref, own_ref, own_limit_ref, own_mass_ref,
+    wide_ref, sums_ref, own_sums_ref, away_ref,
 ):
-    count = out_ref.shape[0]
-    half = core_ref[0] if mine else 1 - core_ref[0]
-    first = pl.multiple_of(half * 512 + skip, 128)
     dual = -SHIFT - joined_lse(parts_ref[...])
     top = jnp.max(dual)
     factor = jnp.exp2(dual - top)
-    lines = slice(skip // 128, (skip + count) // 128)
-    base = jnp.where(half == 0, base_ref[0:4], base_ref[4:8])[lines]
-
-    def keep(start, values):
+    shares = [jnp.broadcast_to(factor[k : k + 1], (16, 128)) for k in range(8)]
+    own = core_ref[0] * 512
+
+    def keep(weights_ref, sums_ref, start, values):
         mass = None
         for k, term in enumerate(values):
             mass = term if mass is None else mass + term
             weights_ref[pl.ds(start, 16), k * 128 : (k + 1) * 128] = term.astype(BF16)
         sums_ref[pl.ds(start, 16), :] = mass
 
-    shares = [jnp.broadcast_to(factor[k : k + 1], (16, 128)) for k in range(8)]
-
-    @pl.loop(0, count // 128)
-    def _(at):
+    def weigh(at, first, weights_ref, sums_ref):
         for q in range(8):
             start = pl.multiple_of(at * 128 + q * 16, 16)
             rows = pl.ds(pl.multiple_of(first + start, 16), 16)
-            keep(start, [terms_ref[rows, k * 128 : (k + 1) * 128] * shares[k] for k in range(8)])
-
-    limit_ref[...] = (top - SHIFT) - base
-    mass_ref[...] = lane_sums(sums_ref[...])
-
-    @pl.when(jnp.min(mass_ref[...]) < TINY)
-    def _():
-        duals = [jnp.broadcast_to(dual[k : k + 1], (16, 128)) for k in range(8)]
-
-        @pl.loop(0, count // 16)
-        def _(at):
-            start = pl.multiple_of(at * 16, 16)
-            rows = pl.ds(pl.multiple_of(first + start, 16), 16)
-            logits = [tile_ref[rows, k * 128 : (k + 1) * 128] + duals[k] for k in range(8)]
-            peak = logits[0]
-            for part in logits[1:]:
-                peak = jnp.maximum(peak, part)
-            peak = jnp.broadcast_to(jnp.max(peak, axis=1, keepdims=True), (16, 128))
-            wide_ref[pl.ds(start, 16), :] = peak
-            keep(start, [jnp.exp2(part - peak) for part in logits])
-
-        limit_ref[...] = to_lanes(wide_ref[...], diagonal())
+            values = [terms_ref[rows, k * 128 : (k + 1) * 128] * shares[k] for k in range(8)]
+            keep(weights_ref, sums_ref, start, values)
+
+    def settle(first, weights_ref, sums_ref, limit_ref, mass_ref):
+        base = jnp.where(first == 0, base_ref[0:4], base_ref[4:8])
+        limit_ref[...] = (top - SHIFT) - base
         mass_ref[...] = lane_sums(sums_ref[...])
 
+        @pl.when(jnp.min(mass_ref[...]) < TINY)
+        def _():
+            duals = [jnp.broadcast_to(dual[k : k + 1], (16, 128)) for k in range(8)]
+
+            @pl.loop(0, 32)
+            def _(at):
+                start = pl.multiple_of(at * 16, 16)
+                rows = pl.ds(pl.multiple_of(first + start, 16), 16)
+                logits = [tile_ref[rows, k * 128 : (k + 1) * 128] + duals[k] for k in range(8)]
+                peak = logits[0]
+                for part in logits[1:]:
+                    peak = jnp.maximum(peak, part)
+                peak = jnp.broadcast_to(jnp.max(peak, axis=1, keepdims=True), (16, 128))
+                wide_ref[pl.ds(start, 16), :] = peak
+                keep(weights_ref, sums_ref, start, [jnp.exp2(part - peak) for part in logits])
+
+            limit_ref[...] = to_lanes(wide_ref[...], diagonal())
+            mass_ref[...] = lane_sums(sums_ref[...])
+
+    @pl.loop(0, 4)
+    def _(at):
+        weigh(at, 512 - own, away_ref, sums_ref)
+
+    settle(512 - own, away_ref, sums_ref, limit_ref, mass_ref)
+
+    @pl.loop(0, 4)
+    def _(at):
+        here = pl.ds(pl.multiple_of(at * 256, 256), 256)
+        weigh(at, own, own_ref, own_sums_ref)
+        out_ref[:, here] = jnp.dot(
+            away_ref[...], block_ref[:, here], preferred_element_type=F32
+        ).astype(BF16)
+
+    settle(own, own_ref, own_sums_ref, own_limit_ref, own_mass_ref)
+
+
+def own_kernel(weights_ref, block_ref, out_ref):
     @pl.loop(0, 4)
     def _(at):
         here = pl.ds(pl.multiple_of(at * 256, 256), 256)
         out_ref[:, here] = jnp.dot(
             weights_ref[...], block_ref[:, here], preferred_element_type=F32
-        ).astype(out_ref.dtype)
+        )
 
 
 def pieces_of(value):
@@ -427,33 +436,28 @@
 
 
 def cores_kernel(
-    skip, mine_ref, limit_ref, mass_ref, other_ref, other_limit_ref, other_mass_ref, out_ref
+    mine_ref, limit_ref, mass_ref, other_ref, other_limit_ref, other_mass_ref, out_ref
 ):
-    count = mine_ref.shape[0]
-    lines = slice(skip // 128, (skip + count) // 128)
-    other_limit, other_mass = other_limit_ref[...][lines], other_mass_ref[...][lines]
-    limit = jnp.maximum(limit_ref[...], other_limit)
-    a, b = jnp.exp2(limit_ref[...] - limit), jnp.exp2(other_limit - limit)
-    mass = a * mass_ref[...] + b * other_mass
-    for k in range(count // 128):
+    limit = jnp.maximum(limit_ref[...], other_limit_ref[...])
+    a, b = jnp.exp2(limit_ref[...] - limit), jnp.exp2(other_limit_ref[...] - limit)
+    mass = a * mass_ref[...] + b * other_mass_ref[...]
+    for k in range(4):
         wide_a, wide_b = to_sublanes(a[k : k + 1]), to_sublanes(b[k : k + 1])
         rows = slice(k * 128, (k + 1) * 128)
-        other_rows = slice(skip + k * 128, skip + (k + 1) * 128)
         for g, block in enumerate(BLOCKS):
             here = slice(block * 128, (block + 1) * 128)
             out_ref[g, rows, :] = (
-                wide_a * mine_ref[rows, here] + wide_b * other_ref[other_rows, here].astype(F32)
+                wide_a * mine_ref[rows, here] + wide_b * other_ref[rows, here].astype(F32)
             ).astype(BF16)
-    pieces = pieces_of(limit) + pieces_of(mass)
-    pieces = jnp.concatenate(pieces + [jnp.zeros_like(pieces[0])] * 2, axis=0)
+    pieces = jnp.concatenate(pieces_of(limit) + pieces_of(mass), axis=0)
     for g in range(8):
-        out_ref[g, count:, :] = pieces
+        out_ref[g, 512:, :] = pieces
 
 
 def groups_kernel(*refs):
     out_ref, start = refs[-1], 0
     for parts_ref in refs[:-1]:
-        count = parts_ref.shape[1] // 136 * 128
+        count = parts_ref.shape[1] // 134 * 128
         n = count // 128
         pieces = parts_ref[:, count:, :].astype(F32)
         limit = pieces[:, 0:n] + pieces[:, n : 2 * n] + pieces[:, 2 * n : 3 * n]
@@ -522,22 +526,19 @@
         compiler_params=pltpu.CompilerParams(vmem_limit_bytes=2 << 20),
     )(noise_draws, noise_pair)
     features = exchanged(spread, "x")
-    rows = call(
-        noise_kernel, jax.ShapeDtypeStruct((512, FEATURES), BF16), scalars=1, arrays=1, limit=4
-    )(place, features)
-    other_rows = moved(rows, "core", 1)
-    block, tile, squared, top, masses, peaks = call(
+    other_features = moved(features, "core", 1)
+    rows, block, tile, squared, top, masses, peaks = call(
         near_kernel,
-        (block_out, tile_out, wide_out, wide_out, wide_out, line),
-        [pltpu.SemaphoreType.DMA],
+        (block_out, block_out, tile_out, wide_out, wide_out, wide_out, line),
+        [pltpu.SemaphoreType.DMA((1,))],
         flops=1 << 30,
         scalars=1,
         arrays=7,
         kept=(3,),
-    )(place, rows, other_rows, *packs)
+    )(place, features, other_features, *packs)
     block, tile, parts = call(
-        far_kernel, (block_out, tile_out, part), [wide], 1 << 30, 1, 13, aliases={12: 0, 13: 1}
-    )(place, rows, other_rows, *far, squared, top, masses, peaks, block, tile)
+        far_kernel, (block_out, tile_out, part), [wide], 1 << 30, 1, 12, aliases={11: 0, 12: 1}
+    )(place, rows, *far, squared, top, masses, peaks, block, tile)
     for sweep in range(ITERS):
         if sweep:
             parts = call(row_kernel, part, [wide], arrays=4)(terms, tile, parts, base)
@@ -551,36 +552,29 @@
         parts = exchanged(parts, COL)
     core = place[4:5]
 
-    def last(mine, skip, count, dtype):
-        lines = jax.ShapeDtypeStruct((count // 128, 128), F32)
-        spare = pltpu.VMEM((count, 128), F32)
-        return call(
-            functools.partial(last_kernel, mine, skip),
-            (jax.ShapeDtypeStruct((count, FEATURES), dtype), lines, lines),
-            [spare, spare, pltpu.VMEM((count, COLS), BF16)],
-            count << 21,
-            1,
-            5,
-        )(core, terms, tile, parts, base, block)
-
-    away = last(False, 0, 512, BF16)
-    other = [moved(value, "core", 1) for value in away]
-    messages, skip = [], 0
-    for count in OWN:
-        own = last(True, skip, count, F32)
-        message = call(
-            functools.partial(cores_kernel, skip),
-            jax.ShapeDtypeStruct((8, count // 128 * 136, 128), BF16),
-            arrays=6,
-        )(*own, *other)
-        messages.append(exchanged(message, OWNERS))
-        skip += count
-    return call(
-        groups_kernel, jax.ShapeDtypeStruct((512, 128), F32), arrays=len(messages)
-    )(*messages)
-
-
-OWN = (512,)
+    half_lines = jax.ShapeDtypeStruct((4, 128), F32)
+    half_wide = pltpu.VMEM((512, 128), F32)
+    half_rows = jax.ShapeDtypeStruct((512, FEATURES), BF16)
+    away, away_limit, away_mass, weights, limit, mass = call(
+        away_kernel,
+        (half_rows, half_lines, half_lines, half_rows, half_lines, half_lines),
+        [half_wide, half_wide, half_wide, pltpu.VMEM((512, COLS), BF16)],
+        1 << 30,
+        1,
+        5,
+    )(core, terms, tile, parts, base, block)
+    other = [moved(value, "core", 1) for value in (away, away_limit, away_mass)]
+    own = call(
+        own_kernel, jax.ShapeDtypeStruct((512, FEATURES), F32), flops=1 << 30, arrays=2
+    )(weights, block)
+    message = call(
+        cores_kernel, jax.ShapeDtypeStruct((8, 536, 128), BF16), arrays=6
+    )(own, limit, mass, *other)
+    return call(groups_kernel, jax.ShapeDtypeStruct((512, 128), F32), arrays=1)(
+        exchanged(message, OWNERS)
+    )
+
+
 PACKS = ((0,), (1, 7), (2, 6), (3, 5), (4,))
 
 

time: 224 us -> 222 us (level)
  blocking collectives: 110 us -> 127 us
  waiting for transfers between devices: 32.6 us -> 16.7 us
  starting transfers between devices: 31.9 us -> 27.5 us
    all_to_all x9 -> x10, blocking collectives: 110 us -> 127 us  [exchanged(): return lax.all_to_all(parts, axes, 0, 0, tiled=True)]
    all_to_all x1 -> x0, waiting for transfers between devices: 12.1 us -> none  [exchanged(): return lax.all_to_all(parts, axes, 0, 0, tiled=True)]
    all_to_all x1 -> x0, starting transfers between devices: 5.6 us -> none  [exchanged(): return lax.all_to_all(parts, axes, 0, 0, tiled=True)]
    ppermute x17, waiting for transfers between devices: 20.5 us -> 16.7 us  [moved(): lax.ppermute(array, axis, [(k, (k + step) % size) for k in range(size)])]
    pallas_call x7 -> x6, Pallas kernels: 22 us -> 21.6 us  [the longest x1 10.3 us: local(): call(away_kernel, (half_rows, half_lines, half_lines, half_rows, half_lin...]
  transfers between devices with their start and end apart: 18 -> 17, of which waited for: 7 -> 7; matrix products, arithmetic and copies ran while one was open for 0% -> 0% of each run, Pallas kernels for 5% -> 4%
where the time goes in v2:
time: 222 us; the launch traced here: 220 us
  blocking collectives  127 us (57%)
  Pallas kernels  48.1 us (22%)
  starting transfers between devices  27.5 us (12%)
  waiting for transfers between devices  16.7 us (8%)
    all_to_all x10, blocking collectives, exchanged(): return lax.all_to_all(parts, axes, 0, 0, tiled=True)  127 us
    ppermute x17, starting transfers between devices, moved(): lax.ppermute(array, axis, [(k, (k + step) % size) for k in range(size)])  27.5 us
    ppermute x17, waiting for transfers between devices, moved(): lax.ppermute(array, axis, [(k, (k + step) % size) for k in range(size)])  16.7 us
    pallas_call x3, Pallas kernels, local(): parts = call(row_kernel, part, [wide], arrays=4)(terms, tile, parts, base)  13.1 us
    pallas_call x1, Pallas kernels, local(): call(away_kernel, (half_rows, half_lines, half_lines, half_rows, half_lin...  10.3 us
    pallas_call x3, Pallas kernels, local(): call(column_kernel, part, [wide], arrays=4)(terms, tile, parts, base)  7.56 us
    pallas_call x1, Pallas kernels, local(): call(near_kernel, (block_out, block_out, tile_out, wide_out, wide_out, wi...  5.02 us
  transfers between devices with their start and end apart: 17, of which 7 were waited for; matrix products, arithmetic and copies ran while one was open for 0% of the time, Pallas kernels for 4%

profile of v2, /device:TPU:2, one launch (start us, length us, event | category | flops | bytes accessed | tf_op | source)
XLA Modules:
  0.0 220.4 jit_solution(3643567555074671939)
XLA Ops:
  1.6 3.9 %collective-permute-done.other_ref = bf16[512,128]{1,0:T(8,128)(2,1)S(1)} collective-permute-done((bf16[512,128]{1,0:T(8,128)(2,1)}, bf16[512,128]{1,0:T(8,128)(2,1)S(1)}, u32[]{:S(2)}, u32[]{:S(2)}) %collective-permute-start) | collective-permute-done | bytes 131104 | tf_op jit(solution)/shard_map/ppermute | solution.py:479
  7.8 17.4 %all_to_all.50.refs_0_ = bf16[4,2,512,128]{3,2,1,0:T(8,128)(2,1)S(1)} all-to-all(bf16[4,2,512,128]{3,2,1,0:T(8,128)(2,1)S(1)} %spread.1), channel_id=1, replica_groups=mesh['y_lo'=2,'x'=4,'y_hi'=2,'z'=8,'core'=2] {'x'}, dimensions={0} | all-to-all | bytes 2097152 | tf_op jit(solution)/shard_map/all_to_all | solution.py:483
  25.2 5.9 %collective-permute-start.3 = (bf16[64,1024]{1,0:T(8,128)(2,1)S(1)}, bf16[64,1024]{1,0:T(8,128)(2,1)S(1)}, u32[]{:S(2)}, u32[]{:S(2)}) collective-permute-start(bf16[64,1024]{1,0:T(8,128)(2,1)S(1)} %copy-done.1), channel_id=1, source_target_pairs={{0,14},{2,0},{4,2},{6,4},{8,6},{10,8},{12,10},{14,12},{1,15},{3,1}... | collective-permute-start | bytes 393224 | tf_op jit(solution)/shard_map/ppermute | solution.py:479
  31.0 3.4 %collective-permute-done.3.refs_1_ = bf16[64,1024]{1,0:T(8,128)(2,1)S(1)} collective-permute-done((bf16[64,1024]{1,0:T(8,128)(2,1)S(1)}, bf16[64,1024]{1,0:T(8,128)(2,1)S(1)}, u32[]{:S(2)}, u32[]{:S(2)}) %collective-permute-start.3) | collective-permute-done | bytes 131104 | tf_op jit(solution)/shard_map/ppermute | solution.py:479
  34.5 3.7 %collective-permute-start.5 = (bf16[64,1024]{1,0:T(8,128)(2,1)S(1)}, bf16[64,1024]{1,0:T(8,128)(2,1)S(1)}, u32[]{:S(2)}, u32[]{:S(2)}) collective-permute-start(bf16[64,1024]{1,0:T(8,128)(2,1)S(1)} %collective-permute-done.3.refs_1_), channel_id=1, source_target_pairs={{0,14},{2,0},{4,2},{6,4},{8,6},{10,8},{12,10},{14,12},{1,15},{3,1}... | collective-permute-start | bytes 393224 | tf_op jit(solution)/shard_map/ppermute | solution.py:479
  38.2 2.6 %collective-permute-done.5.refs_1_ = bf16[64,1024]{1,0:T(8,128)(2,1)S(1)} collective-permute-done((bf16[64,1024]{1,0:T(8,128)(2,1)S(1)}, bf16[64,1024]{1,0:T(8,128)(2,1)S(1)}, u32[]{:S(2)}, u32[]{:S(2)}) %collective-permute-start.5) | collective-permute-done | bytes 131104 | tf_op jit(solution)/shard_map/ppermute | solution.py:479
  40.7 3.7 %collective-permute-start.7 = (bf16[64,1024]{1,0:T(8,128)(2,1)S(1)}, bf16[64,1024]{1,0:T(8,128)(2,1)S(1)}, u32[]{:S(2)}, u32[]{:S(2)}) collective-permute-start(bf16[64,1024]{1,0:T(8,128)(2,1)S(1)} %collective-permute-done.5.refs_1_), channel_id=1, source_target_pairs={{0,14},{2,0},{4,2},{6,4},{8,6},{10,8},{12,10},{14,12},{1,15},{3,1}... | collective-permute-start | bytes 393224 | tf_op jit(solution)/shard_map/ppermute | solution.py:479
  44.5 3.3 %collective-permute-start.10 = (bf16[128,1024]{1,0:T(8,128)(2,1)S(1)}, bf16[128,1024]{1,0:T(8,128)(2,1)S(1)}, u32[]{:S(2)}, u32[]{:S(2)}) collective-permute-start(bf16[128,1024]{1,0:T(8,128)(2,1)S(1)} %shard_map.28.refs_3_), channel_id=1, source_target_pairs={{0,16},{16,0},{1,17},{17,1},{2,18},{18,2},{3,19},{19,3},{4,20},{20... | collective-permute-start | bytes 786440 | tf_op jit(solution)/shard_map/ppermute | solution.py:479
  50.1 2.7 %collective-permute-done.6.refs_0_ = bf16[64,1024]{1,0:T(8,128)(2,1)S(1)} collective-permute-done((bf16[64,1024]{1,0:T(8,128)(2,1)S(1)}, bf16[64,1024]{1,0:T(8,128)(2,1)S(1)}, u32[]{:S(2)}, u32[]{:S(2)}) %collective-permute-start.6) | collective-permute-done | bytes 131104 | tf_op jit(solution)/shard_map/ppermute | solution.py:479
  53.5 3.6 %collective-permute-start.12 = (bf16[128,1024]{1,0:T(8,128)(2,1)}, bf16[128,1024]{1,0:T(8,128)(2,1)S(1)}, u32[]{:S(2)}, u32[]{:S(2)}) collective-permute-start(bf16[128,1024]{1,0:T(8,128)(2,1)} %shard_map.30.refs_5_), channel_id=1, source_target_pairs={{0,16},{16,0},{1,17},{17,1},{2,18},{18,2},{3,19},{19,3},{4,20},{20... | collective-permute-start | bytes 786440 | tf_op jit(solution)/shard_map/ppermute | solution.py:479
  57.9 2.8 %collective-permute-start.13 = (bf16[64,1024]{1,0:T(8,128)(2,1)}, bf16[64,1024]{1,0:T(8,128)(2,1)S(1)}, u32[]{:S(2)}, u32[]{:S(2)}) collective-permute-start(bf16[64,1024]{1,0:T(8,128)(2,1)} %collective-permute-done.8.refs_6_), channel_id=1, source_target_pairs={{0,16},{16,0},{1,17},{17,1},{2,18},{18,2},{3,19},{19,3},{4,20},{20... | collective-permute-start | bytes 393224 | tf_op jit(solution)/shard_map/ppermute | solution.py:479
  60.7 5.0 %shard_map.31 = (bf16[1024,1024]{1,0:T(8,128)(2,1)S(1)}, bf16[1024,1024]{1,0:T(8,128)(2,1)S(1)}, f32[1024,1024]{1,0:T(8,128)S(1)}, f32[1024,128]{1,0:T(8,128)S(1...) custom-call(s32[5]{0:T(128)S(1)} %stack.23.place_ref, ...), custom_call_target="tpu_custom_call" | custom-call | flops 1073741824 | bytes 4194304 | tf_op jit(solution)/shard_map/pallas_call | solution.py:530
  65.8 2.5 %collective-permute-done.9.refs_0_ = bf16[64,1024]{1,0:T(8,128)(2,1)S(1)} collective-permute-done((bf16[64,1024]{1,0:T(8,128)(2,1)S(1)}, bf16[64,1024]{1,0:T(8,128)(2,1)S(1)}, u32[]{:S(2)}, u32[]{:S(2)}) %collective-permute-start.9) | collective-permute-done | bytes 131104 | tf_op jit(solution)/shard_map/ppermute | solution.py:479
  69.6 2.7 %shard_map.32 = (bf16[1024,1024]{1,0:T(8,128)(2,1)S(1)}, f32[1024,1024]{1,0:T(8,128)S(1)}, f32[16,8,128]{2,1,0:T(8,128)S(1)}) custom-call(s32[5]{0:T(128)S(1)} %stack.23.place_ref, bf16[1024,1024]{1,0:T(8,128)(2,1)S(1)} %get-tuple-element.24.rows_ref, ...), custom_call_target="tpu_custom_call", output_to_operand_aliasing={{0}: (11, {}), {1}: (12, {})} | custom-call | flops 1073741824 | bytes 4194304 | tf_op jit(solution)/shard_map/pallas_call | solution.py:539
  72.4 9.5 %all_to_all.51.parts_ref = f32[16,8,128]{2,1,0:T(8,128)S(1)} all-to-all(f32[16,8,128]{2,1,0:T(8,128)S(1)} %get-tuple-element.32), channel_id=1, replica_groups=mesh['y_lo'=2,'x'=4,'y_hi'=2,'z'=8,'core'=2] {'y_lo','x','core'}, dimensions={0} | all-to-all | bytes 131072 | tf_op jit(solution)/shard_map/all_to_all | solution.py:483
  81.8 3.0 %shard_map.33 = (f32[16,8,128]{2,1,0:T(8,128)S(1)}, f32[8,128]{1,0:T(8,128)S(1)}, f32[1024,1024]{1,0:T(8,128)S(1)}) custom-call(f32[1024,1024]{1,0:T(8,128)S(1)} %get-tuple-element.31.tile_ref, f32[16,8,128]{2,1,0:T(8,128)S(1)} %all_to_all.51.parts_ref), custom_call_target="tpu_custom_call" | custom-call | bytes 4194304 | tf_op jit(solution)/shard_map/pallas_call | solution.py:549
  84.8 16.5 %all_to_all.52.parts_ref = f32[16,8,128]{2,1,0:T(8,128)S(1)} all-to-all(f32[16,8,128]{2,1,0:T(8,128)S(1)} %get-tuple-element.34), channel_id=1, replica_groups=mesh['y_lo'=2,'x'=4,'y_hi'=2,'z'=8,'core'=2] {'y_hi','z'}, dimensions={0} | all-to-all | bytes 131072 | tf_op jit(solution)/shard_map/all_to_all | solution.py:483
  101.3 4.4 %shard_map.34 = f32[16,8,128]{2,1,0:T(8,128)S(1)} custom-call(f32[1024,1024]{1,0:T(8,128)S(1)} %get-tuple-element.33.terms_ref, f32[1024,1024]{1,0:T(8,128)S(1)} %get-tuple-element.31.tile_ref, f32[16,8,128]{2,1,0:T(8,128)S(1)} %all_to_all.52.parts_ref, f32[8,128]{1,0:T(8,128)S(1)} %get-tuple-element.35.base_ref), custom_call_target="tpu_custom_call" | custom-call | bytes 4194304 | tf_op jit(solution)/shard_map/pallas_call | solution.py:544
  105.7 8.7 %all_to_all.53.parts_ref = f32[16,8,128]{2,1,0:T(8,128)S(1)} all-to-all(f32[16,8,128]{2,1,0:T(8,128)S(1)} %shard_map.34), channel_id=1, replica_groups=mesh['y_lo'=2,'x'=4,'y_hi'=2,'z'=8,'core'=2] {'y_lo','x','core'}, dimensions={0} | all-to-all | bytes 131072 | tf_op jit(solution)/shard_map/all_to_all | solution.py:483
  114.4 2.5 %shard_map.35 = f32[16,8,128]{2,1,0:T(8,128)S(1)} custom-call(f32[1024,1024]{1,0:T(8,128)S(1)} %get-tuple-element.33.terms_ref, f32[1024,1024]{1,0:T(8,128)S(1)} %get-tuple-element.31.tile_ref, f32[16,8,128]{2,1,0:T(8,128)S(1)} %all_to_all.53.parts_ref, f32[8,128]{1,0:T(8,128)S(1)} %get-tuple-element.35.base_ref), custom_call_target="tpu_custom_call" | custom-call | bytes 4194304 | tf_op jit(solution)/shard_map/pallas_call | solution.py:547
  117.0 12.6 %all_to_all.54.parts_ref = f32[16,8,128]{2,1,0:T(8,128)S(1)} all-to-all(f32[16,8,128]{2,1,0:T(8,128)S(1)} %shard_map.35), channel_id=1, replica_groups=mesh['y_lo'=2,'x'=4,'y_hi'=2,'z'=8,'core'=2] {'y_hi','z'}, dimensions={0} | all-to-all | bytes 131072 | tf_op jit(solution)/shard_map/all_to_all | solution.py:483
  129.6 4.4 %shard_map.36 = f32[16,8,128]{2,1,0:T(8,128)S(1)} custom-call(f32[1024,1024]{1,0:T(8,128)S(1)} %get-tuple-element.33.terms_ref, f32[1024,1024]{1,0:T(8,128)S(1)} %get-tuple-element.31.tile_ref, f32[16,8,128]{2,1,0:T(8,128)S(1)} %all_to_all.54.parts_ref, f32[8,128]{1,0:T(8,128)S(1)} %get-tuple-element.35.base_ref), custom_call_target="tpu_custom_call" | custom-call | bytes 4194304 | tf_op jit(solution)/shard_map/pallas_call | solution.py:544
  134.0 8.7 %all_to_all.55.parts_ref = f32[16,8,128]{2,1,0:T(8,128)S(1)} all-to-all(f32[16,8,128]{2,1,0:T(8,128)S(1)} %shard_map.36), channel_id=1, replica_groups=mesh['y_lo'=2,'x'=4,'y_hi'=2,'z'=8,'core'=2] {'y_lo','x','core'}, dimensions={0} | all-to-all | bytes 131072 | tf_op jit(solution)/shard_map/all_to_all | solution.py:483
  142.7 2.5 %shard_map.37 = f32[16,8,128]{2,1,0:T(8,128)S(1)} custom-call(f32[1024,1024]{1,0:T(8,128)S(1)} %get-tuple-element.33.terms_ref, f32[1024,1024]{1,0:T(8,128)S(1)} %get-tuple-element.31.tile_ref, f32[16,8,128]{2,1,0:T(8,128)S(1)} %all_to_all.55.parts_ref, f32[8,128]{1,0:T(8,128)S(1)} %get-tuple-element.35.base_ref), custom_call_target="tpu_custom_call" | custom-call | bytes 4194304 | tf_op jit(solution)/shard_map/pallas_call | solution.py:547
  145.2 12.9 %all_to_all.56.parts_ref = f32[16,8,128]{2,1,0:T(8,128)S(1)} all-to-all(f32[16,8,128]{2,1,0:T(8,128)S(1)} %shard_map.37), channel_id=1, replica_groups=mesh['y_lo'=2,'x'=4,'y_hi'=2,'z'=8,'core'=2] {'y_hi','z'}, dimensions={0} | all-to-all | bytes 131072 | tf_op jit(solution)/shard_map/all_to_all | solution.py:483
  158.1 4.4 %shard_map.38 = f32[16,8,128]{2,1,0:T(8,128)S(1)} custom-call(f32[1024,1024]{1,0:T(8,128)S(1)} %get-tuple-element.33.terms_ref, f32[1024,1024]{1,0:T(8,128)S(1)} %get-tuple-element.31.tile_ref, f32[16,8,128]{2,1,0:T(8,128)S(1)} %all_to_all.56.parts_ref, f32[8,128]{1,0:T(8,128)S(1)} %get-tuple-element.35.base_ref), custom_call_target="tpu_custom_call" | custom-call | bytes 4194304 | tf_op jit(solution)/shard_map/pallas_call | solution.py:544
  162.5 8.7 %all_to_all.57.parts_ref = f32[16,8,128]{2,1,0:T(8,128)S(1)} all-to-all(f32[16,8,128]{2,1,0:T(8,128)S(1)} %shard_map.38), channel_id=1, replica_groups=mesh['y_lo'=2,'x'=4,'y_hi'=2,'z'=8,'core'=2] {'y_lo','x','core'}, dimensions={0} | all-to-all | bytes 131072 | tf_op jit(solution)/shard_map/all_to_all | solution.py:483
  171.2 2.5 %shard_map.39 = f32[16,8,128]{2,1,0:T(8,128)S(1)} custom-call(f32[1024,1024]{1,0:T(8,128)S(1)} %get-tuple-element.33.terms_ref, f32[1024,1024]{1,0:T(8,128)S(1)} %get-tuple-element.31.tile_ref, f32[16,8,128]{2,1,0:T(8,128)S(1)} %all_to_all.57.parts_ref, f32[8,128]{1,0:T(8,128)S(1)} %get-tuple-element.35.base_ref), custom_call_target="tpu_custom_call" | custom-call | bytes 4194304 | tf_op jit(solution)/shard_map/pallas_call | solution.py:547
  173.7 12.6 %all_to_all.58.parts_ref = f32[16,8,128]{2,1,0:T(8,128)S(1)} all-to-all(f32[16,8,128]{2,1,0:T(8,128)S(1)} %shard_map.39), channel_id=1, replica_groups=mesh['y_lo'=2,'x'=4,'y_hi'=2,'z'=8,'core'=2] {'y_hi','z'}, dimensions={0} | all-to-all | bytes 131072 | tf_op jit(solution)/shard_map/all_to_all | solution.py:483
  186.3 10.3 %shard_map.40 = (bf16[512,1024]{1,0:T(8,128)(2,1)S(1)}, f32[4,128]{1,0:T(4,128)S(1)}, f32[4,128]{1,0:T(4,128)S(1)}, bf16[512,1024]{1,0:T(8,128)(2,1)S(1)}, f32[4,128]{1,0:T(4,128)S(1)}, /*index=5*/f32[4,128]{1,0:T(4,128)S(1)}) custom-call(s32[1]{0:T(128)} %bitcast.core_ref, f32[1024,1024]{1,0:T(8,128)S(1)} %get-tuple-element.33.terms_ref, ...), custom_call_target="tpu_custom_call" | custom-call | flops 1073741824 | bytes 4194304 | tf_op jit(solution)/shard_map/pallas_call | solution.py:558
  197.2 1.8 shard_map.41.mine_ref
  199.7 19.3 %all_to_all.59.refs_0_ = bf16[8,536,128]{2,1,0:T(8,128)(2,1)S(1)} all-to-all(bf16[8,536,128]{2,1,0:T(8,128)(2,1)S(1)} %shard_map.42), channel_id=1, replica_groups=mesh['y_lo'=2,'x'=4,'y_hi'=2,'z'=8,'core'=2] {'x','y_lo'}, dimensions={0} | all-to-all | bytes 2195456 | tf_op jit(solution)/shard_map/all_to_all | solution.py:483
  (34 shorter events, 11.9 us)
Async XLA Ops:
  0.0 5.4 %collective-permute-start = (bf16[512,128]{1,0:T(8,128)(2,1)}, bf16[512,128]{1,0:T(8,128)(2,1)S(1)}, u32[]{:S(2)}, u32[]{:S(2)}) collective-permute-start(bf16[512,128]{1,0:T(8,128)(2,1)} %noise_ref.1), channel_id=1, source_target_pairs={{0,128},{128,0},{1,129},{129,1},{2,130},{130,2},{3,131},{131,3},{4... | collective-permute-start | bytes 393224 | tf_op jit(solution)/shard_map/ppermute | solution.py:479
  5.4 0.9 copy-start
  6.4 18.8 %copy-start.1 = (bf16[64,1024]{1,0:T(8,128)(2,1)S(1)}, bf16[64,1024]{1,0:T(8,128)(2,1)}, u32[]{:S(2)}) copy-start(bf16[64,1024]{1,0:T(8,128)(2,1)} %refs_2_.1) | copy-start | bytes 393220
  25.2 32.7 %collective-permute-start.1 = (bf16[4,2,512,128]{3,2,1,0:T(8,128)(2,1)S(1)}, bf16[4,2,512,128]{3,2,1,0:T(8,128)(2,1)S(1)}, u32[]{:S(2)}, u32[]{:S(2)}) collective-permute-start(bf16[4,2,512,128]{3,2,1,0:T(8,128)(2,1)S(1)} %all_to_all.50.refs_0_), channel_id=1, source_target_pairs={{0,1},{1,0},{2,3},{3,2},{4,5},{5,4},{6,7},{7,6},{8,9},{9,8},{10,11... | collective-permute-start | bytes 3145736 | tf_op jit(solution)/shard_map/ppermute | solution.py:479
  25.2 9.3 %collective-permute-start.3 = (bf16[64,1024]{1,0:T(8,128)(2,1)S(1)}, bf16[64,1024]{1,0:T(8,128)(2,1)S(1)}, u32[]{:S(2)}, u32[]{:S(2)}) collective-permute-start(bf16[64,1024]{1,0:T(8,128)(2,1)S(1)} %copy-done.1), channel_id=1, source_target_pairs={{0,14},{2,0},{4,2},{6,4},{8,6},{10,8},{12,10},{14,12},{1,15},{3,1}... | collective-permute-start | bytes 393224 | tf_op jit(solution)/shard_map/ppermute | solution.py:479
  31.0 7.1 %collective-permute-start.2 = (bf16[64,1024]{1,0:T(8,128)(2,1)S(1)}, bf16[64,1024]{1,0:T(8,128)(2,1)S(1)}, u32[]{:S(2)}, u32[]{:S(2)}) collective-permute-start(bf16[64,1024]{1,0:T(8,128)(2,1)S(1)} %copy-done.1), channel_id=1, source_target_pairs={{0,2},{2,4},{4,6},{6,8},{8,10},{10,12},{12,14},{14,0},{1,3},{3,5},... | collective-permute-start | bytes 393224 | tf_op jit(solution)/shard_map/ppermute | solution.py:479
  34.5 6.3 %collective-permute-start.5 = (bf16[64,1024]{1,0:T(8,128)(2,1)S(1)}, bf16[64,1024]{1,0:T(8,128)(2,1)S(1)}, u32[]{:S(2)}, u32[]{:S(2)}) collective-permute-start(bf16[64,1024]{1,0:T(8,128)(2,1)S(1)} %collective-permute-done.3.refs_1_), channel_id=1, source_target_pairs={{0,14},{2,0},{4,2},{6,4},{8,6},{10,8},{12,10},{14,12},{1,15},{3,1}... | collective-permute-start | bytes 393224 | tf_op jit(solution)/shard_map/ppermute | solution.py:479
  38.2 6.3 %collective-permute-start.4 = (bf16[64,1024]{1,0:T(8,128)(2,1)S(1)}, bf16[64,1024]{1,0:T(8,128)(2,1)S(1)}, u32[]{:S(2)}, u32[]{:S(2)}) collective-permute-start(bf16[64,1024]{1,0:T(8,128)(2,1)S(1)} %collective-permute-done.2.refs_0_), channel_id=1, source_target_pairs={{0,2},{2,4},{4,6},{6,8},{8,10},{10,12},{12,14},{14,0},{1,3},{3,5},... | collective-permute-start | bytes 393224 | tf_op jit(solution)/shard_map/ppermute | solution.py:479
  40.7 7.7 %collective-permute-start.7 = (bf16[64,1024]{1,0:T(8,128)(2,1)S(1)}, bf16[64,1024]{1,0:T(8,128)(2,1)S(1)}, u32[]{:S(2)}, u32[]{:S(2)}) collective-permute-start(bf16[64,1024]{1,0:T(8,128)(2,1)S(1)} %collective-permute-done.5.refs_1_), channel_id=1, source_target_pairs={{0,14},{2,0},{4,2},{6,4},{8,6},{10,8},{12,10},{14,12},{1,15},{3,1}... | collective-permute-start | bytes 393224 | tf_op jit(solution)/shard_map/ppermute | solution.py:479
  44.4 8.4 %collective-permute-start.6 = (bf16[64,1024]{1,0:T(8,128)(2,1)S(1)}, bf16[64,1024]{1,0:T(8,128)(2,1)S(1)}, u32[]{:S(2)}, u32[]{:S(2)}) collective-permute-start(bf16[64,1024]{1,0:T(8,128)(2,1)S(1)} %collective-permute-done.4.refs_0_), channel_id=1, source_target_pairs={{0,2},{2,4},{4,6},{6,8},{8,10},{10,12},{12,14},{14,0},{1,3},{3,5},... | collective-permute-start | bytes 393224 | tf_op jit(solution)/shard_map/ppermute | solution.py:479
  44.5 23.8 %collective-permute-start.10 = (bf16[128,1024]{1,0:T(8,128)(2,1)S(1)}, bf16[128,1024]{1,0:T(8,128)(2,1)S(1)}, u32[]{:S(2)}, u32[]{:S(2)}) collective-permute-start(bf16[128,1024]{1,0:T(8,128)(2,1)S(1)} %shard_map.28.refs_3_), channel_id=1, source_target_pairs={{0,16},{16,0},{1,17},{17,1},{2,18},{18,2},{3,19},{19,3},{4,20},{20... | collective-permute-start | bytes 786440 | tf_op jit(solution)/shard_map/ppermute | solution.py:479
  47.7 9.4 %collective-permute-start.8 = (bf16[64,1024]{1,0:T(8,128)(2,1)S(1)}, bf16[64,1024]{1,0:T(8,128)(2,1)}, u32[]{:S(2)}, u32[]{:S(2)}) collective-permute-start(bf16[64,1024]{1,0:T(8,128)(2,1)S(1)} %collective-permute-done.4.refs_0_), channel_id=1, source_target_pairs={{0,4},{2,6},{4,8},{6,10},{8,12},{10,14},{12,0},{14,2},{1,5},{3,7},... | collective-permute-start | bytes 393224 | tf_op jit(solution)/shard_map/ppermute | solution.py:479
  48.5 21.2 %collective-permute-start.11 = (bf16[128,1024]{1,0:T(8,128)(2,1)}, bf16[128,1024]{1,0:T(8,128)(2,1)S(1)}, u32[]{:S(2)}, u32[]{:S(2)}) collective-permute-start(bf16[128,1024]{1,0:T(8,128)(2,1)} %shard_map.29.refs_4_), channel_id=1, source_target_pairs={{0,16},{16,0},{1,17},{17,1},{2,18},{18,2},{3,19},{19,3},{4,20},{20... | collective-permute-start | bytes 786440 | tf_op jit(solution)/shard_map/ppermute | solution.py:479
  53.5 16.1 %collective-permute-start.12 = (bf16[128,1024]{1,0:T(8,128)(2,1)}, bf16[128,1024]{1,0:T(8,128)(2,1)S(1)}, u32[]{:S(2)}, u32[]{:S(2)}) collective-permute-start(bf16[128,1024]{1,0:T(8,128)(2,1)} %shard_map.30.refs_5_), channel_id=1, source_target_pairs={{0,16},{16,0},{1,17},{17,1},{2,18},{18,2},{3,19},{19,3},{4,20},{20... | collective-permute-start | bytes 786440 | tf_op jit(solution)/shard_map/ppermute | solution.py:479
  57.1 11.1 %collective-permute-start.9 = (bf16[64,1024]{1,0:T(8,128)(2,1)S(1)}, bf16[64,1024]{1,0:T(8,128)(2,1)S(1)}, u32[]{:S(2)}, u32[]{:S(2)}) collective-permute-start(bf16[64,1024]{1,0:T(8,128)(2,1)S(1)} %copy-done.1), channel_id=1, source_target_pairs={{0,16},{16,0},{1,17},{17,1},{2,18},{18,2},{3,19},{19,3},{4,20},{20... | collective-permute-start | bytes 393224 | tf_op jit(solution)/shard_map/ppermute | solution.py:479
  57.9 11.8 %collective-permute-start.13 = (bf16[64,1024]{1,0:T(8,128)(2,1)}, bf16[64,1024]{1,0:T(8,128)(2,1)S(1)}, u32[]{:S(2)}, u32[]{:S(2)}) collective-permute-start(bf16[64,1024]{1,0:T(8,128)(2,1)} %collective-permute-done.8.refs_6_), channel_id=1, source_target_pairs={{0,16},{16,0},{1,17},{17,1},{2,18},{18,2},{3,19},{19,3},{4,20},{20... | collective-permute-start | bytes 393224 | tf_op jit(solution)/shard_map/ppermute | solution.py:479
  196.6 2.7 %collective-permute-start.14 = (bf16[512,1024]{1,0:T(8,128)(2,1)S(1)}, bf16[512,1024]{1,0:T(8,128)(2,1)S(1)}, u32[]{:S(2)}, u32[]{:S(2)}) collective-permute-start(bf16[512,1024]{1,0:T(8,128)(2,1)S(1)} %get-tuple-element.40), channel_id=1, source_target_pairs={{0,1},{1,0},{2,3},{3,2},{4,5},{5,4},{6,7},{7,6},{8,9},{9,8},{10,11... | collective-permute-start | bytes 3145736 | tf_op jit(solution)/shard_map/ppermute | solution.py:479
  196.6 2.7 %collective-permute-start.15 = (f32[4,128]{1,0:T(4,128)S(1)}, f32[4,128]{1,0:T(4,128)S(1)}, u32[]{:S(2)}, u32[]{:S(2)}) collective-permute-start(f32[4,128]{1,0:T(4,128)S(1)} %get-tuple-element.41), channel_id=1, source_target_pairs={{0,1},{1,0},{2,3},{3,2},{4,5},{5,4},{6,7},{7,6},{8,9},{9,8},{10,11... | collective-permute-start | bytes 6152 | tf_op jit(solution)/shard_map/ppermute | solution.py:479
  197.1 2.2 collective-permute-start.16

commit v3 on v2

--- a/solution.py
+++ b/solution.py
@@ -279,21 +279,6 @@
             at = group * 8 + jnp.bitwise_and(z - back + 8, 7)
             rows = pl.ds(pl.multiple_of(at * 64, 64), 64)
             block_ref[rows, :] = pack[k * 64 : (k + 1) * 64, :]
-
-
-def first_masses(tile_ref, base, top_ref, sums_ref):
-    @pl.loop(0, ROWS // STEP)
-    def _(at):
-        for q in range(STEP // 8):
-            rows = pl.ds(pl.multiple_of(at * STEP + q * 8, 8), 8)
-            top = jnp.broadcast_to(jnp.max(top_ref[rows, :], axis=1, keepdims=True), (8, 128))
-            top_ref[rows, :] = top
-            mass = None
-            for k in range(4):
-                cols = pl.ds(pl.multiple_of(base + k * 128, 128), 128)
-                term = jnp.exp2(tile_ref[rows, cols] - top)
-                mass = term if mass is None else mass + term
-            sums_ref[rows, :] = mass
 
 
 def near_kernel(place_ref, *refs):
@@ -321,11 +306,16 @@
     base = pl.multiple_of(y_hi * 512, 512)
 
     def use(at, pair):
-        top = jnp.maximum(*pair)
-        top_ref[...] = jnp.maximum(jnp.where(at == 0, top, top_ref[...]), top)
+        @pl.when(at == 0)
+        def _():
+            peak = jnp.max(jnp.maximum(*pair), axis=1, keepdims=True)
+            top_ref[...] = jnp.broadcast_to(peak, (ROWS, 128))
+            sums_ref[...] = jnp.zeros((ROWS, 128), F32)
+
+        top = top_ref[...]
+        sums_ref[...] = sums_ref[...] + (jnp.exp2(pair[0] - top) + jnp.exp2(pair[1] - top))
 
     costs(rows_ref, block_ref, tile_ref, squares_ref, base, use)
-    first_masses(tile_ref, base, top_ref, sums_ref)
     line_ref[...] = to_lanes(top_ref[...], diagonal())
 
 

time: 222 us -> 222 us (level)
  no operation moved by 1% of the time
where the time goes in v3:
time: 222 us; the launch traced here: 220 us
  blocking collectives  127 us (57%)
  Pallas kernels  47.8 us (22%)
  starting transfers between devices  27.5 us (12%)
  waiting for transfers between devices  17 us (8%)
    all_to_all x10, blocking collectives, exchanged(): return lax.all_to_all(parts, axes, 0, 0, tiled=True)  127 us
    ppermute x17, starting transfers between devices, moved(): lax.ppermute(array, axis, [(k, (k + step) % size) for k in range(size)])  27.5 us
    ppermute x17, waiting for transfers between devices, moved(): lax.ppermute(array, axis, [(k, (k + step) % size) for k in range(size)])  17 us
    pallas_call x3, Pallas kernels, local(): parts = call(row_kernel, part, [wide], arrays=4)(terms, tile, parts, base)  13.1 us
    pallas_call x1, Pallas kernels, local(): call(away_kernel, (half_rows, half_lines, half_lines, half_rows, half_lin...  10.3 us
    pallas_call x3, Pallas kernels, local(): call(column_kernel, part, [wide], arrays=4)(terms, tile, parts, base)  7.56 us
    pallas_call x1, Pallas kernels, local(): call(near_kernel, (block_out, block_out, tile_out, wide_out, wide_out, wi...  4.7 us
  transfers between devices with their start and end apart: 17, of which 7 were waited for; matrix products, arithmetic and copies ran while one was open for 0% of the time, Pallas kernels for 4%

profile of v3, /device:TPU:2, one launch (start us, length us, event | category | flops | bytes accessed | tf_op | source)
XLA Modules:
  0.0 220.4 jit_solution(1588052362878622932)
XLA Ops:
  1.6 3.9 %collective-permute-done.other_ref = bf16[512,128]{1,0:T(8,128)(2,1)S(1)} collective-permute-done((bf16[512,128]{1,0:T(8,128)(2,1)}, bf16[512,128]{1,0:T(8,128)(2,1)S(1)}, u32[]{:S(2)}, u32[]{:S(2)}) %collective-permute-start) | collective-permute-done | bytes 131104 | tf_op jit(solution)/shard_map/ppermute | solution.py:469
  7.8 17.4 %all_to_all.50.refs_0_ = bf16[4,2,512,128]{3,2,1,0:T(8,128)(2,1)S(1)} all-to-all(bf16[4,2,512,128]{3,2,1,0:T(8,128)(2,1)S(1)} %spread.1), channel_id=1, replica_groups=mesh['y_lo'=2,'x'=4,'y_hi'=2,'z'=8,'core'=2] {'x'}, dimensions={0} | all-to-all | bytes 2097152 | tf_op jit(solution)/shard_map/all_to_all | solution.py:473
  25.2 5.9 %collective-permute-start.3 = (bf16[64,1024]{1,0:T(8,128)(2,1)S(1)}, bf16[64,1024]{1,0:T(8,128)(2,1)S(1)}, u32[]{:S(2)}, u32[]{:S(2)}) collective-permute-start(bf16[64,1024]{1,0:T(8,128)(2,1)S(1)} %copy-done.1), channel_id=1, source_target_pairs={{0,14},{2,0},{4,2},{6,4},{8,6},{10,8},{12,10},{14,12},{1,15},{3,1}... | collective-permute-start | bytes 393224 | tf_op jit(solution)/shard_map/ppermute | solution.py:469
  31.0 3.4 %collective-permute-done.3.refs_1_ = bf16[64,1024]{1,0:T(8,128)(2,1)S(1)} collective-permute-done((bf16[64,1024]{1,0:T(8,128)(2,1)S(1)}, bf16[64,1024]{1,0:T(8,128)(2,1)S(1)}, u32[]{:S(2)}, u32[]{:S(2)}) %collective-permute-start.3) | collective-permute-done | bytes 131104 | tf_op jit(solution)/shard_map/ppermute | solution.py:469
  34.5 3.7 %collective-permute-start.5 = (bf16[64,1024]{1,0:T(8,128)(2,1)S(1)}, bf16[64,1024]{1,0:T(8,128)(2,1)S(1)}, u32[]{:S(2)}, u32[]{:S(2)}) collective-permute-start(bf16[64,1024]{1,0:T(8,128)(2,1)S(1)} %collective-permute-done.3.refs_1_), channel_id=1, source_target_pairs={{0,14},{2,0},{4,2},{6,4},{8,6},{10,8},{12,10},{14,12},{1,15},{3,1}... | collective-permute-start | bytes 393224 | tf_op jit(solution)/shard_map/ppermute | solution.py:469
  38.2 2.6 %collective-permute-done.5.refs_1_ = bf16[64,1024]{1,0:T(8,128)(2,1)S(1)} collective-permute-done((bf16[64,1024]{1,0:T(8,128)(2,1)S(1)}, bf16[64,1024]{1,0:T(8,128)(2,1)S(1)}, u32[]{:S(2)}, u32[]{:S(2)}) %collective-permute-start.5) | collective-permute-done | bytes 131104 | tf_op jit(solution)/shard_map/ppermute | solution.py:469
  40.7 3.7 %collective-permute-start.7 = (bf16[64,1024]{1,0:T(8,128)(2,1)S(1)}, bf16[64,1024]{1,0:T(8,128)(2,1)S(1)}, u32[]{:S(2)}, u32[]{:S(2)}) collective-permute-start(bf16[64,1024]{1,0:T(8,128)(2,1)S(1)} %collective-permute-done.5.refs_1_), channel_id=1, source_target_pairs={{0,14},{2,0},{4,2},{6,4},{8,6},{10,8},{12,10},{14,12},{1,15},{3,1}... | collective-permute-start | bytes 393224 | tf_op jit(solution)/shard_map/ppermute | solution.py:469
  44.5 3.3 %collective-permute-start.10 = (bf16[128,1024]{1,0:T(8,128)(2,1)S(1)}, bf16[128,1024]{1,0:T(8,128)(2,1)S(1)}, u32[]{:S(2)}, u32[]{:S(2)}) collective-permute-start(bf16[128,1024]{1,0:T(8,128)(2,1)S(1)} %shard_map.28.refs_3_), channel_id=1, source_target_pairs={{0,16},{16,0},{1,17},{17,1},{2,18},{18,2},{3,19},{19,3},{4,20},{20... | collective-permute-start | bytes 786440 | tf_op jit(solution)/shard_map/ppermute | solution.py:469
  50.1 2.7 %collective-permute-done.6.refs_0_ = bf16[64,1024]{1,0:T(8,128)(2,1)S(1)} collective-permute-done((bf16[64,1024]{1,0:T(8,128)(2,1)S(1)}, bf16[64,1024]{1,0:T(8,128)(2,1)S(1)}, u32[]{:S(2)}, u32[]{:S(2)}) %collective-permute-start.6) | collective-permute-done | bytes 131104 | tf_op jit(solution)/shard_map/ppermute | solution.py:469
  53.5 3.6 %collective-permute-start.12 = (bf16[128,1024]{1,0:T(8,128)(2,1)}, bf16[128,1024]{1,0:T(8,128)(2,1)S(1)}, u32[]{:S(2)}, u32[]{:S(2)}) collective-permute-start(bf16[128,1024]{1,0:T(8,128)(2,1)} %shard_map.30.refs_5_), channel_id=1, source_target_pairs={{0,16},{16,0},{1,17},{17,1},{2,18},{18,2},{3,19},{19,3},{4,20},{20... | collective-permute-start | bytes 786440 | tf_op jit(solution)/shard_map/ppermute | solution.py:469
  57.9 2.8 %collective-permute-start.13 = (bf16[64,1024]{1,0:T(8,128)(2,1)}, bf16[64,1024]{1,0:T(8,128)(2,1)S(1)}, u32[]{:S(2)}, u32[]{:S(2)}) collective-permute-start(bf16[64,1024]{1,0:T(8,128)(2,1)} %collective-permute-done.8.refs_6_), channel_id=1, source_target_pairs={{0,16},{16,0},{1,17},{17,1},{2,18},{18,2},{3,19},{19,3},{4,20},{20... | collective-permute-start | bytes 393224 | tf_op jit(solution)/shard_map/ppermute | solution.py:469
  60.7 4.7 %shard_map.31 = (bf16[1024,1024]{1,0:T(8,128)(2,1)S(1)}, bf16[1024,1024]{1,0:T(8,128)(2,1)S(1)}, f32[1024,1024]{1,0:T(8,128)S(1)}, f32[1024,128]{1,0:T(8,128)S(1...) custom-call(s32[5]{0:T(128)S(1)} %stack.23.place_ref, ...), custom_call_target="tpu_custom_call" | custom-call | flops 1073741824 | bytes 4194304 | tf_op jit(solution)/shard_map/pallas_call | solution.py:520
  65.4 2.8 %collective-permute-done.9.refs_0_ = bf16[64,1024]{1,0:T(8,128)(2,1)S(1)} collective-permute-done((bf16[64,1024]{1,0:T(8,128)(2,1)S(1)}, bf16[64,1024]{1,0:T(8,128)(2,1)S(1)}, u32[]{:S(2)}, u32[]{:S(2)}) %collective-permute-start.9) | collective-permute-done | bytes 131104 | tf_op jit(solution)/shard_map/ppermute | solution.py:469
  69.6 2.7 %shard_map.32 = (bf16[1024,1024]{1,0:T(8,128)(2,1)S(1)}, f32[1024,1024]{1,0:T(8,128)S(1)}, f32[16,8,128]{2,1,0:T(8,128)S(1)}) custom-call(s32[5]{0:T(128)S(1)} %stack.23.place_ref, bf16[1024,1024]{1,0:T(8,128)(2,1)S(1)} %get-tuple-element.24.rows_ref, ...), custom_call_target="tpu_custom_call", output_to_operand_aliasing={{0}: (11, {}), {1}: (12, {})} | custom-call | flops 1073741824 | bytes 4194304 | tf_op jit(solution)/shard_map/pallas_call | solution.py:529
  72.4 9.5 %all_to_all.51.parts_ref = f32[16,8,128]{2,1,0:T(8,128)S(1)} all-to-all(f32[16,8,128]{2,1,0:T(8,128)S(1)} %get-tuple-element.32), channel_id=1, replica_groups=mesh['y_lo'=2,'x'=4,'y_hi'=2,'z'=8,'core'=2] {'y_lo','x','core'}, dimensions={0} | all-to-all | bytes 131072 | tf_op jit(solution)/shard_map/all_to_all | solution.py:473
  81.8 3.0 %shard_map.33 = (f32[16,8,128]{2,1,0:T(8,128)S(1)}, f32[8,128]{1,0:T(8,128)S(1)}, f32[1024,1024]{1,0:T(8,128)S(1)}) custom-call(f32[1024,1024]{1,0:T(8,128)S(1)} %get-tuple-element.31.tile_ref, f32[16,8,128]{2,1,0:T(8,128)S(1)} %all_to_all.51.parts_ref), custom_call_target="tpu_custom_call" | custom-call | bytes 4194304 | tf_op jit(solution)/shard_map/pallas_call | solution.py:539
  84.8 16.5 %all_to_all.52.parts_ref = f32[16,8,128]{2,1,0:T(8,128)S(1)} all-to-all(f32[16,8,128]{2,1,0:T(8,128)S(1)} %get-tuple-element.34), channel_id=1, replica_groups=mesh['y_lo'=2,'x'=4,'y_hi'=2,'z'=8,'core'=2] {'y_hi','z'}, dimensions={0} | all-to-all | bytes 131072 | tf_op jit(solution)/shard_map/all_to_all | solution.py:473
  101.3 4.4 %shard_map.34 = f32[16,8,128]{2,1,0:T(8,128)S(1)} custom-call(f32[1024,1024]{1,0:T(8,128)S(1)} %get-tuple-element.33.terms_ref, f32[1024,1024]{1,0:T(8,128)S(1)} %get-tuple-element.31.tile_ref, f32[16,8,128]{2,1,0:T(8,128)S(1)} %all_to_all.52.parts_ref, f32[8,128]{1,0:T(8,128)S(1)} %get-tuple-element.35.base_ref), custom_call_target="tpu_custom_call" | custom-call | bytes 4194304 | tf_op jit(solution)/shard_map/pallas_call | solution.py:534
  105.7 8.7 %all_to_all.53.parts_ref = f32[16,8,128]{2,1,0:T(8,128)S(1)} all-to-all(f32[16,8,128]{2,1,0:T(8,128)S(1)} %shard_map.34), channel_id=1, replica_groups=mesh['y_lo'=2,'x'=4,'y_hi'=2,'z'=8,'core'=2] {'y_lo','x','core'}, dimensions={0} | all-to-all | bytes 131072 | tf_op jit(solution)/shard_map/all_to_all | solution.py:473
  114.4 2.5 %shard_map.35 = f32[16,8,128]{2,1,0:T(8,128)S(1)} custom-call(f32[1024,1024]{1,0:T(8,128)S(1)} %get-tuple-element.33.terms_ref, f32[1024,1024]{1,0:T(8,128)S(1)} %get-tuple-element.31.tile_ref, f32[16,8,128]{2,1,0:T(8,128)S(1)} %all_to_all.53.parts_ref, f32[8,128]{1,0:T(8,128)S(1)} %get-tuple-element.35.base_ref), custom_call_target="tpu_custom_call" | custom-call | bytes 4194304 | tf_op jit(solution)/shard_map/pallas_call | solution.py:537
  117.0 12.6 %all_to_all.54.parts_ref = f32[16,8,128]{2,1,0:T(8,128)S(1)} all-to-all(f32[16,8,128]{2,1,0:T(8,128)S(1)} %shard_map.35), channel_id=1, replica_groups=mesh['y_lo'=2,'x'=4,'y_hi'=2,'z'=8,'core'=2] {'y_hi','z'}, dimensions={0} | all-to-all | bytes 131072 | tf_op jit(solution)/shard_map/all_to_all | solution.py:473
  129.6 4.4 %shard_map.36 = f32[16,8,128]{2,1,0:T(8,128)S(1)} custom-call(f32[1024,1024]{1,0:T(8,128)S(1)} %get-tuple-element.33.terms_ref, f32[1024,1024]{1,0:T(8,128)S(1)} %get-tuple-element.31.tile_ref, f32[16,8,128]{2,1,0:T(8,128)S(1)} %all_to_all.54.parts_ref, f32[8,128]{1,0:T(8,128)S(1)} %get-tuple-element.35.base_ref), custom_call_target="tpu_custom_call" | custom-call | bytes 4194304 | tf_op jit(solution)/shard_map/pallas_call | solution.py:534
  134.0 8.7 %all_to_all.55.parts_ref = f32[16,8,128]{2,1,0:T(8,128)S(1)} all-to-all(f32[16,8,128]{2,1,0:T(8,128)S(1)} %shard_map.36), channel_id=1, replica_groups=mesh['y_lo'=2,'x'=4,'y_hi'=2,'z'=8,'core'=2] {'y_lo','x','core'}, dimensions={0} | all-to-all | bytes 131072 | tf_op jit(solution)/shard_map/all_to_all | solution.py:473
  142.7 2.5 %shard_map.37 = f32[16,8,128]{2,1,0:T(8,128)S(1)} custom-call(f32[1024,1024]{1,0:T(8,128)S(1)} %get-tuple-element.33.terms_ref, f32[1024,1024]{1,0:T(8,128)S(1)} %get-tuple-element.31.tile_ref, f32[16,8,128]{2,1,0:T(8,128)S(1)} %all_to_all.55.parts_ref, f32[8,128]{1,0:T(8,128)S(1)} %get-tuple-element.35.base_ref), custom_call_target="tpu_custom_call" | custom-call | bytes 4194304 | tf_op jit(solution)/shard_map/pallas_call | solution.py:537
  145.2 12.9 %all_to_all.56.parts_ref = f32[16,8,128]{2,1,0:T(8,128)S(1)} all-to-all(f32[16,8,128]{2,1,0:T(8,128)S(1)} %shard_map.37), channel_id=1, replica_groups=mesh['y_lo'=2,'x'=4,'y_hi'=2,'z'=8,'core'=2] {'y_hi','z'}, dimensions={0} | all-to-all | bytes 131072 | tf_op jit(solution)/shard_map/all_to_all | solution.py:473
  158.1 4.4 %shard_map.38 = f32[16,8,128]{2,1,0:T(8,128)S(1)} custom-call(f32[1024,1024]{1,0:T(8,128)S(1)} %get-tuple-element.33.terms_ref, f32[1024,1024]{1,0:T(8,128)S(1)} %get-tuple-element.31.tile_ref, f32[16,8,128]{2,1,0:T(8,128)S(1)} %all_to_all.56.parts_ref, f32[8,128]{1,0:T(8,128)S(1)} %get-tuple-element.35.base_ref), custom_call_target="tpu_custom_call" | custom-call | bytes 4194304 | tf_op jit(solution)/shard_map/pallas_call | solution.py:534
  162.5 8.7 %all_to_all.57.parts_ref = f32[16,8,128]{2,1,0:T(8,128)S(1)} all-to-all(f32[16,8,128]{2,1,0:T(8,128)S(1)} %shard_map.38), channel_id=1, replica_groups=mesh['y_lo'=2,'x'=4,'y_hi'=2,'z'=8,'core'=2] {'y_lo','x','core'}, dimensions={0} | all-to-all | bytes 131072 | tf_op jit(solution)/shard_map/all_to_all | solution.py:473
  171.2 2.5 %shard_map.39 = f32[16,8,128]{2,1,0:T(8,128)S(1)} custom-call(f32[1024,1024]{1,0:T(8,128)S(1)} %get-tuple-element.33.terms_ref, f32[1024,1024]{1,0:T(8,128)S(1)} %get-tuple-element.31.tile_ref, f32[16,8,128]{2,1,0:T(8,128)S(1)} %all_to_all.57.parts_ref, f32[8,128]{1,0:T(8,128)S(1)} %get-tuple-element.35.base_ref), custom_call_target="tpu_custom_call" | custom-call | bytes 4194304 | tf_op jit(solution)/shard_map/pallas_call | solution.py:537
  173.7 12.6 %all_to_all.58.parts_ref = f32[16,8,128]{2,1,0:T(8,128)S(1)} all-to-all(f32[16,8,128]{2,1,0:T(8,128)S(1)} %shard_map.39), channel_id=1, replica_groups=mesh['y_lo'=2,'x'=4,'y_hi'=2,'z'=8,'core'=2] {'y_hi','z'}, dimensions={0} | all-to-all | bytes 131072 | tf_op jit(solution)/shard_map/all_to_all | solution.py:473
  186.3 10.3 %shard_map.40 = (bf16[512,1024]{1,0:T(8,128)(2,1)S(1)}, f32[4,128]{1,0:T(4,128)S(1)}, f32[4,128]{1,0:T(4,128)S(1)}, bf16[512,1024]{1,0:T(8,128)(2,1)S(1)}, f32[4,128]{1,0:T(4,128)S(1)}, /*index=5*/f32[4,128]{1,0:T(4,128)S(1)}) custom-call(s32[1]{0:T(128)} %bitcast.core_ref, f32[1024,1024]{1,0:T(8,128)S(1)} %get-tuple-element.33.terms_ref, ...), custom_call_target="tpu_custom_call" | custom-call | flops 1073741824 | bytes 4194304 | tf_op jit(solution)/shard_map/pallas_call | solution.py:548
  197.2 1.8 shard_map.41.mine_ref
  199.7 19.3 %all_to_all.59.refs_0_ = bf16[8,536,128]{2,1,0:T(8,128)(2,1)S(1)} all-to-all(bf16[8,536,128]{2,1,0:T(8,128)(2,1)S(1)} %shard_map.42), channel_id=1, replica_groups=mesh['y_lo'=2,'x'=4,'y_hi'=2,'z'=8,'core'=2] {'x','y_lo'}, dimensions={0} | all-to-all | bytes 2195456 | tf_op jit(solution)/shard_map/all_to_all | solution.py:473
  (34 shorter events, 11.9 us)
Async XLA Ops:
  0.0 5.4 %collective-permute-start = (bf16[512,128]{1,0:T(8,128)(2,1)}, bf16[512,128]{1,0:T(8,128)(2,1)S(1)}, u32[]{:S(2)}, u32[]{:S(2)}) collective-permute-start(bf16[512,128]{1,0:T(8,128)(2,1)} %noise_ref.1), channel_id=1, source_target_pairs={{0,128},{128,0},{1,129},{129,1},{2,130},{130,2},{3,131},{131,3},{4... | collective-permute-start | bytes 393224 | tf_op jit(solution)/shard_map/ppermute | solution.py:469
  5.4 0.9 copy-start
  6.4 18.8 %copy-start.1 = (bf16[64,1024]{1,0:T(8,128)(2,1)S(1)}, bf16[64,1024]{1,0:T(8,128)(2,1)}, u32[]{:S(2)}) copy-start(bf16[64,1024]{1,0:T(8,128)(2,1)} %refs_2_.1) | copy-start | bytes 393220
  25.2 32.7 %collective-permute-start.1 = (bf16[4,2,512,128]{3,2,1,0:T(8,128)(2,1)S(1)}, bf16[4,2,512,128]{3,2,1,0:T(8,128)(2,1)S(1)}, u32[]{:S(2)}, u32[]{:S(2)}) collective-permute-start(bf16[4,2,512,128]{3,2,1,0:T(8,128)(2,1)S(1)} %all_to_all.50.refs_0_), channel_id=1, source_target_pairs={{0,1},{1,0},{2,3},{3,2},{4,5},{5,4},{6,7},{7,6},{8,9},{9,8},{10,11... | collective-permute-start | bytes 3145736 | tf_op jit(solution)/shard_map/ppermute | solution.py:469
  25.2 9.3 %collective-permute-start.3 = (bf16[64,1024]{1,0:T(8,128)(2,1)S(1)}, bf16[64,1024]{1,0:T(8,128)(2,1)S(1)}, u32[]{:S(2)}, u32[]{:S(2)}) collective-permute-start(bf16[64,1024]{1,0:T(8,128)(2,1)S(1)} %copy-done.1), channel_id=1, source_target_pairs={{0,14},{2,0},{4,2},{6,4},{8,6},{10,8},{12,10},{14,12},{1,15},{3,1}... | collective-permute-start | bytes 393224 | tf_op jit(solution)/shard_map/ppermute | solution.py:469
  31.0 7.1 %collective-permute-start.2 = (bf16[64,1024]{1,0:T(8,128)(2,1)S(1)}, bf16[64,1024]{1,0:T(8,128)(2,1)S(1)}, u32[]{:S(2)}, u32[]{:S(2)}) collective-permute-start(bf16[64,1024]{1,0:T(8,128)(2,1)S(1)} %copy-done.1), channel_id=1, source_target_pairs={{0,2},{2,4},{4,6},{6,8},{8,10},{10,12},{12,14},{14,0},{1,3},{3,5},... | collective-permute-start | bytes 393224 | tf_op jit(solution)/shard_map/ppermute | solution.py:469
  34.5 6.3 %collective-permute-start.5 = (bf16[64,1024]{1,0:T(8,128)(2,1)S(1)}, bf16[64,1024]{1,0:T(8,128)(2,1)S(1)}, u32[]{:S(2)}, u32[]{:S(2)}) collective-permute-start(bf16[64,1024]{1,0:T(8,128)(2,1)S(1)} %collective-permute-done.3.refs_1_), channel_id=1, source_target_pairs={{0,14},{2,0},{4,2},{6,4},{8,6},{10,8},{12,10},{14,12},{1,15},{3,1}... | collective-permute-start | bytes 393224 | tf_op jit(solution)/shard_map/ppermute | solution.py:469
  38.2 6.3 %collective-permute-start.4 = (bf16[64,1024]{1,0:T(8,128)(2,1)S(1)}, bf16[64,1024]{1,0:T(8,128)(2,1)S(1)}, u32[]{:S(2)}, u32[]{:S(2)}) collective-permute-start(bf16[64,1024]{1,0:T(8,128)(2,1)S(1)} %collective-permute-done.2.refs_0_), channel_id=1, source_target_pairs={{0,2},{2,4},{4,6},{6,8},{8,10},{10,12},{12,14},{14,0},{1,3},{3,5},... | collective-permute-start | bytes 393224 | tf_op jit(solution)/shard_map/ppermute | solution.py:469
  40.7 7.7 %collective-permute-start.7 = (bf16[64,1024]{1,0:T(8,128)(2,1)S(1)}, bf16[64,1024]{1,0:T(8,128)(2,1)S(1)}, u32[]{:S(2)}, u32[]{:S(2)}) collective-permute-start(bf16[64,1024]{1,0:T(8,128)(2,1)S(1)} %collective-permute-done.5.refs_1_), channel_id=1, source_target_pairs={{0,14},{2,0},{4,2},{6,4},{8,6},{10,8},{12,10},{14,12},{1,15},{3,1}... | collective-permute-start | bytes 393224 | tf_op jit(solution)/shard_map/ppermute | solution.py:469
  44.4 8.4 %collective-permute-start.6 = (bf16[64,1024]{1,0:T(8,128)(2,1)S(1)}, bf16[64,1024]{1,0:T(8,128)(2,1)S(1)}, u32[]{:S(2)}, u32[]{:S(2)}) collective-permute-start(bf16[64,1024]{1,0:T(8,128)(2,1)S(1)} %collective-permute-done.4.refs_0_), channel_id=1, source_target_pairs={{0,2},{2,4},{4,6},{6,8},{8,10},{10,12},{12,14},{14,0},{1,3},{3,5},... | collective-permute-start | bytes 393224 | tf_op jit(solution)/shard_map/ppermute | solution.py:469
  44.5 23.8 %collective-permute-start.10 = (bf16[128,1024]{1,0:T(8,128)(2,1)S(1)}, bf16[128,1024]{1,0:T(8,128)(2,1)S(1)}, u32[]{:S(2)}, u32[]{:S(2)}) collective-permute-start(bf16[128,1024]{1,0:T(8,128)(2,1)S(1)} %shard_map.28.refs_3_), channel_id=1, source_target_pairs={{0,16},{16,0},{1,17},{17,1},{2,18},{18,2},{3,19},{19,3},{4,20},{20... | collective-permute-start | bytes 786440 | tf_op jit(solution)/shard_map/ppermute | solution.py:469
  47.7 9.4 %collective-permute-start.8 = (bf16[64,1024]{1,0:T(8,128)(2,1)S(1)}, bf16[64,1024]{1,0:T(8,128)(2,1)}, u32[]{:S(2)}, u32[]{:S(2)}) collective-permute-start(bf16[64,1024]{1,0:T(8,128)(2,1)S(1)} %collective-permute-done.4.refs_0_), channel_id=1, source_target_pairs={{0,4},{2,6},{4,8},{6,10},{8,12},{10,14},{12,0},{14,2},{1,5},{3,7},... | collective-permute-start | bytes 393224 | tf_op jit(solution)/shard_map/ppermute | solution.py:469
  48.5 21.2 %collective-permute-start.11 = (bf16[128,1024]{1,0:T(8,128)(2,1)}, bf16[128,1024]{1,0:T(8,128)(2,1)S(1)}, u32[]{:S(2)}, u32[]{:S(2)}) collective-permute-start(bf16[128,1024]{1,0:T(8,128)(2,1)} %shard_map.29.refs_4_), channel_id=1, source_target_pairs={{0,16},{16,0},{1,17},{17,1},{2,18},{18,2},{3,19},{19,3},{4,20},{20... | collective-permute-start | bytes 786440 | tf_op jit(solution)/shard_map/ppermute | solution.py:469
  53.5 16.1 %collective-permute-start.12 = (bf16[128,1024]{1,0:T(8,128)(2,1)}, bf16[128,1024]{1,0:T(8,128)(2,1)S(1)}, u32[]{:S(2)}, u32[]{:S(2)}) collective-permute-start(bf16[128,1024]{1,0:T(8,128)(2,1)} %shard_map.30.refs_5_), channel_id=1, source_target_pairs={{0,16},{16,0},{1,17},{17,1},{2,18},{18,2},{3,19},{19,3},{4,20},{20... | collective-permute-start | bytes 786440 | tf_op jit(solution)/shard_map/ppermute | solution.py:469
  57.1 11.1 %collective-permute-start.9 = (bf16[64,1024]{1,0:T(8,128)(2,1)S(1)}, bf16[64,1024]{1,0:T(8,128)(2,1)S(1)}, u32[]{:S(2)}, u32[]{:S(2)}) collective-permute-start(bf16[64,1024]{1,0:T(8,128)(2,1)S(1)} %copy-done.1), channel_id=1, source_target_pairs={{0,16},{16,0},{1,17},{17,1},{2,18},{18,2},{3,19},{19,3},{4,20},{20... | collective-permute-start | bytes 393224 | tf_op jit(solution)/shard_map/ppermute | solution.py:469
  57.9 11.8 %collective-permute-start.13 = (bf16[64,1024]{1,0:T(8,128)(2,1)}, bf16[64,1024]{1,0:T(8,128)(2,1)S(1)}, u32[]{:S(2)}, u32[]{:S(2)}) collective-permute-start(bf16[64,1024]{1,0:T(8,128)(2,1)} %collective-permute-done.8.refs_6_), channel_id=1, source_target_pairs={{0,16},{16,0},{1,17},{17,1},{2,18},{18,2},{3,19},{19,3},{4,20},{20... | collective-permute-start | bytes 393224 | tf_op jit(solution)/shard_map/ppermute | solution.py:469
  196.6 2.7 %collective-permute-start.14 = (bf16[512,1024]{1,0:T(8,128)(2,1)S(1)}, bf16[512,1024]{1,0:T(8,128)(2,1)S(1)}, u32[]{:S(2)}, u32[]{:S(2)}) collective-permute-start(bf16[512,1024]{1,0:T(8,128)(2,1)S(1)} %get-tuple-element.40), channel_id=1, source_target_pairs={{0,1},{1,0},{2,3},{3,2},{4,5},{5,4},{6,7},{7,6},{8,9},{9,8},{10,11... | collective-permute-start | bytes 3145736 | tf_op jit(solution)/shard_map/ppermute | solution.py:469
  196.6 2.7 %collective-permute-start.15 = (f32[4,128]{1,0:T(4,128)S(1)}, f32[4,128]{1,0:T(4,128)S(1)}, u32[]{:S(2)}, u32[]{:S(2)}) collective-permute-start(f32[4,128]{1,0:T(4,128)S(1)} %get-tuple-element.41), channel_id=1, source_target_pairs={{0,1},{1,0},{2,3},{3,2},{4,5},{5,4},{6,7},{7,6},{8,9},{9,8},{10,11... | collective-permute-start | bytes 6152 | tf_op jit(solution)/shard_map/ppermute | solution.py:469
  197.1 2.2 collective-permute-start.16
